TPU v7x, 768 devices: a whole 4x8x12 slice. The times are simulated.
768 devices in a mesh: lon: 24 (over y_hi, z), lat: 32 (over x, y_lo, core).
Axes of the slice: x: 4, y: 8 (y_hi: 2, y_lo: 4; y = y_hi * 4 + y_lo), z: 12, core: 2. Of those that a mesh axis runs over, the one named last changes fastest.
Arguments:
- increment: float32 [4, 32, 256, 3072], P(None, None, 'lat', 'lon'), may hold values from -6 to 6
- coef_lon: float32 [4, 256, 3072], P(None, 'lat', 'lon'), may hold values from 0.4 to 0.49
- coef_lat: float32 [4, 256, 3072], P(None, 'lat', 'lon'), may hold values from 0.4 to 0.49
- obs_values: float32 [393216, 128], P(('lon', 'lat')), may hold values from -1.8 to 1.8
- obs_weight: float32 [393216, 128], P(('lon', 'lat')), may hold values from 0.25 to 4
- obs_operator: float32 [3, 128, 128], replicated, may hold values from -0.5 to 0.5
- obs_columns: int32 [393216], P(('lon', 'lat')), may hold values from 0 to 1023
- obs_types: int32 [393216], P(('lon', 'lat')), may hold values from 0 to 2
- obs_counts: int32 [24576], P(('lon', 'lat')), may hold values from 0 to 16, as said below
Outputs:
- gradient: float32 [4, 32, 256, 3072], P(None, None, 'lat', 'lon')
- departures: float32 [393216, 128], P(('lon', 'lat'))
Inputs may be any that keep to these rules, and one draw needn't show every extreme that they name: `obs_counts`: each entry counts the live slots of one bucket of 16; slots at or past the count are ignored. In every longitude block some owner latitude block receives full buckets from every source. `obs_columns`: the column within the owner's block, row times 128 plus column. `obs_types`: 0 radiosonde, 1 occultation, 2 radiance.
All inputs are finite; a program needn't handle non-finite values.
Results may differ from a plain program's by a relative error of at most 0.000073.
Values sent between devices are 32-bit elements; how exact they have to be, the bound alone decides.
A program may use at most 32 MiB of HBM per device.

v0:
```python
import jax
import jax.numpy as jnp
from jax import lax
from jax.sharding import PartitionSpec as P

STEPS = 4


SIGN_TABLE = (1.0, 1.0, -1.0, -1.0)


def with_halo(shard, sides, width, wrap):
    for axis, dim in sides:
        peers, length = (lax.axis_size(axis), shard.shape[dim])
        up = [(i, (i + 1) % peers) for i in range(peers if wrap else peers - 1)]
        down = [(j, i) for i, j in up]
        last = lax.slice_in_dim(shard, length - width, length, axis=dim)
        first = lax.slice_in_dim(shard, 0, width, axis=dim)
        before = lax.ppermute(last, axis, up)
        after = lax.ppermute(first, axis, down)
        shard = jnp.concatenate([before, shard, after], axis=dim)
    return shard


def from_behind(shard, axis, by):
    peers = lax.axis_size(axis)
    return lax.ppermute(shard, axis, [(i, (i + by) % peers) for i in range(peers)])


def spread_once(field_state, root_lon, root_lat):
    lon_count = lax.axis_size("lon")
    lat_count = lax.axis_size("lat")
    lat_index = lax.axis_index("lat")
    scaled_lon = root_lon * field_state
    padded_lon = with_halo(scaled_lon, (("lon", 3),), 1, True)
    second_lon = padded_lon[..., 2:] + padded_lon[..., :-2] - 2.0 * scaled_lon
    scaled_lat = root_lat * field_state
    padded_lat = with_halo(scaled_lat, (("lat", 2),), 1, False)
    edge_rows = jnp.stack((scaled_lat[:, :, 0, :], scaled_lat[:, :, -1, :]))
    mirrored = from_behind(edge_rows, "lon", lon_count // 2)
    mirrored = mirrored * jnp.array(SIGN_TABLE, jnp.float32)[:, None, None]
    south_rim = jnp.where(lat_index == 0, mirrored[0], padded_lat[:, :, 0, :])
    north_rim = jnp.where(lat_index == lat_count - 1, mirrored[1], padded_lat[:, :, -1, :])
    padded_lat = padded_lat.at[:, :, 0, :].set(south_rim).at[:, :, -1, :].set(north_rim)
    second_lat = padded_lat[:, :, 2:, :] + padded_lat[:, :, :-2, :] - 2.0 * scaled_lat
    return field_state + root_lon * second_lon + root_lat * second_lat


def diffuse(grid_state, coef_lon, coef_lat):
    root_lon = coef_lon[:, None]
    root_lat = coef_lat[:, None]
    for turn in range(STEPS):
        grid_state = spread_once(grid_state, root_lon, root_lat)
    return grid_state


def decode(slot_code):
    live = slot_code >= 0
    nonneg = jnp.maximum(slot_code, 0)
    return (live, nonneg // 3, nonneg % 3)


def pick_kind(kinds, results):
    return jnp.where(
        (kinds == 0)[:, None], results[0], jnp.where((kinds == 1)[:, None], results[1], results[2])
    )


def observe(live, columns, kinds, observed, weights, obs_operator):
    highest = lax.Precision.HIGHEST
    model = pick_kind(
        kinds, [jnp.dot(columns, obs_operator[kind], precision=highest) for kind in range(3)]
    )
    departures = jnp.where(live[:, None], observed - model, jnp.float32(0.0))
    weighted = weights * departures
    adjoint = pick_kind(
        kinds, [jnp.dot(weighted, obs_operator[kind].T, precision=highest) for kind in range(3)]
    )
    return (departures, adjoint)


def local(
    increment,
    coef_lon,
    coef_lat,
    obs_values,
    obs_weight,
    obs_operator,
    obs_columns,
    obs_types,
    obs_counts,
):
    lat_count = lax.axis_size("lat")
    slot_total = obs_columns.shape[0]
    bucket_size = slot_total // lat_count
    profile_width = increment.shape[0] * increment.shape[1]
    slot_index = jnp.arange(slot_total, dtype=jnp.int32) % bucket_size
    slot_limit = jnp.repeat(obs_counts, bucket_size)
    slot_code = jnp.where(slot_index < slot_limit, obs_columns * 3 + obs_types, -1)
    forcing = jnp.zeros((profile_width, increment.shape[2] * increment.shape[3]), jnp.float32)
    observed_in, weights_in, code_in = (
        lax.all_to_all(obs_values, "lat", split_axis=0, concat_axis=0, tiled=True),
        lax.all_to_all(obs_weight, "lat", split_axis=0, concat_axis=0, tiled=True),
        lax.all_to_all(slot_code, "lat", split_axis=0, concat_axis=0, tiled=True),
    )
    state = diffuse(increment, coef_lon, coef_lat)
    flat_state = state.reshape(profile_width, -1)
    live_in, cell_in, kinds_in = decode(code_in)
    columns = flat_state[:, cell_in].T
    owner_departures, adjoint = observe(
        live_in, columns, kinds_in, observed_in, weights_in, obs_operator
    )
    forcing = forcing.at[:, cell_in].add(adjoint.T)
    departures = lax.all_to_all(owner_departures, "lat", split_axis=0, concat_axis=0, tiled=True)
    smoothed = diffuse(forcing.reshape(increment.shape), coef_lon, coef_lat)
    return (increment - smoothed, departures)


def solution(mesh):
    return jax.shard_map(
        local,
        mesh=mesh,
        in_specs=(
            P(None, None, "lat", "lon"),
            P(None, "lat", "lon"),
            P(None, "lat", "lon"),
            P(("lon", "lat"), None),
            P(("lon", "lat"), None),
            P(),
            P(("lon", "lat")),
            P(("lon", "lat")),
            P(("lon", "lat")),
        ),
        out_specs=(P(None, None, "lat", "lon"), P(("lon", "lat"), None)),
        check_vma=False,
    )
```

profile of v0, /device:TPU:1, one launch (start us, length us, event | category | flops | bytes accessed | tf_op | source)
XLA Modules:
  0.0 439.1 jit_solution(4251603327081085856)
XLA Ops:
  2.8 14.1 %all-to-all-start = ((s32[32,16,1]{1,2,0:T(1,128)}), s32[32,16,1]{1,2,0:T(1,128)S(1)}, u32[]{:S(2)}, u32[]{:S(2)}) async-start(s32[32,16,1]{1,2,0:T(1,128)} %bitcast), calls=%async_computation | async-start | bytes 32768 | tf_op jit(solution)/shard_map/all_to_all | solution.py:104
  26.6 14.4 %collective-permute-start = (f32[4,32,8,1]{3,1,0,2:T(8,128)S(1)}, f32[4,32,8,1]{3,1,0,2:T(8,128)}, u32[]{:S(2)}, u32[]{:S(2)}) collective-permute-start(f32[4,32,8,1]{3,1,0,2:T(8,128)S(1)} %get-tuple-element.244), channel_id=1, source_target_pairs={{32,0},{64,32},{96,64},{128,96},{160,128},{192,160},{224,192},{256... | collective-permute-start | bytes 12296 | tf_op jit(solution)/shard_map/ppermute | solution.py:20
  42.9 10.2 %all-to-all-start.2 = ((f32[32,16,128]{2,1,0:T(8,128)}), f32[32,16,128]{2,1,0:T(8,128)S(1)}, u32[]{:S(2)}, u32[]{:S(2)}) async-start(f32[32,16,128]{2,1,0:T(8,128)} %bitcast.4), calls=%async_computation.2 | async-start | bytes 524288 | tf_op jit(solution)/shard_map/all_to_all | solution.py:102
  55.5 6.8 %collective-permute-done = f32[4,32,8,1]{3,1,0,2:T(8,128)} collective-permute-done((f32[4,32,8,1]{3,1,0,2:T(8,128)S(1)}, f32[4,32,8,1]{3,1,0,2:T(8,128)}, u32[]{:S(2)}, u32[]{:S(2)}) %collective-permute-start) | collective-permute-done | bytes 4128 | tf_op jit(solution)/shard_map/ppermute | solution.py:20
  62.3 12.7 %collective-permute-done.1 = f32[4,32,8,1]{3,1,0,2:T(8,128)} collective-permute-done((f32[4,32,8,1]{3,1,0,2:T(8,128)S(1)}, f32[4,32,8,1]{3,1,0,2:T(8,128)}, u32[]{:S(2)}, u32[]{:S(2)}) %collective-permute-start.1) | collective-permute-done | bytes 4128 | tf_op jit(solution)/shard_map/ppermute | solution.py:19
  82.3 4.8 %collective-permute-start.9 = (f32[2,4,32,128]{3,2,1,0:T(8,128)S(1)}, f32[2,4,32,128]{3,2,1,0:T(8,128)S(1)}, u32[]{:S(2)}, u32[]{:S(2)}) collective-permute-start(f32[2,4,32,128]{3,2,1,0:T(8,128)S(1)} %pad_maximum_fusion.25), channel_id=1, source_target_pairs={{0,384},{32,416},{64,448},{96,480},{128,512},{160,544},{192,576},{... | collective-permute-start | bytes 393224 | tf_op jit(solution)/shard_map/ppermute | solution.py:27
  95.5 14.7 %collective-permute-done.5 = f32[4,32,8,1]{3,1,0,2:T(8,128)S(1)} collective-permute-done((f32[4,32,8,1]{3,1,0,2:T(8,128)S(1)}, f32[4,32,8,1]{3,1,0,2:T(8,128)S(1)}, u32[]{:S(2)}, u32[]{:S(2)}) %collective-permute-start.5) | collective-permute-done | bytes 4128 | tf_op jit(solution)/shard_map/ppermute | solution.py:20
  110.3 10.0 %collective-permute-done.6 = f32[4,32,8,1]{3,1,0,2:T(8,128)S(1)} collective-permute-done((f32[4,32,8,1]{3,1,0,2:T(8,128)S(1)}, f32[4,32,8,1]{3,1,0,2:T(8,128)S(1)}, u32[]{:S(2)}, u32[]{:S(2)}) %collective-permute-start.6) | collective-permute-done | bytes 4128 | tf_op jit(solution)/shard_map/ppermute | solution.py:19
  126.5 5.9 %collective-permute-start.14 = (f32[2,4,32,128]{3,2,1,0:T(8,128)S(1)}, f32[2,4,32,128]{3,2,1,0:T(8,128)S(1)}, u32[]{:S(2)}, u32[]{:S(2)}) collective-permute-start(f32[2,4,32,128]{3,2,1,0:T(8,128)S(1)} %pad_maximum_fusion.26), channel_id=1, source_target_pairs={{0,384},{32,416},{64,448},{96,480},{128,512},{160,544},{192,576},{... | collective-permute-start | bytes 393224 | tf_op jit(solution)/shard_map/ppermute | solution.py:27
  138.1 17.0 %collective-permute-done.10 = f32[4,32,8,1]{3,1,0,2:T(8,128)S(1)} collective-permute-done((f32[4,32,8,1]{3,1,0,2:T(8,128)S(1)}, f32[4,32,8,1]{3,1,0,2:T(8,128)S(1)}, u32[]{:S(2)}, u32[]{:S(2)}) %collective-permute-start.10) | collective-permute-done | bytes 4128 | tf_op jit(solution)/shard_map/ppermute | solution.py:20
  155.1 12.4 %collective-permute-done.11 = f32[4,32,8,1]{3,1,0,2:T(8,128)S(1)} collective-permute-done((f32[4,32,8,1]{3,1,0,2:T(8,128)S(1)}, f32[4,32,8,1]{3,1,0,2:T(8,128)S(1)}, u32[]{:S(2)}, u32[]{:S(2)}) %collective-permute-start.11) | collective-permute-done | bytes 4128 | tf_op jit(solution)/shard_map/ppermute | solution.py:19
  181.5 15.8 %collective-permute-done.15 = f32[4,32,8,1]{3,1,0,2:T(8,128)S(1)} collective-permute-done((f32[4,32,8,1]{3,1,0,2:T(8,128)S(1)}, f32[4,32,8,1]{3,1,0,2:T(8,128)S(1)}, u32[]{:S(2)}, u32[]{:S(2)}) %collective-permute-start.15) | collective-permute-done | bytes 4128 | tf_op jit(solution)/shard_map/ppermute | solution.py:20
  197.4 11.6 %collective-permute-done.16 = f32[4,32,8,1]{3,1,0,2:T(8,128)S(1)} collective-permute-done((f32[4,32,8,1]{3,1,0,2:T(8,128)S(1)}, f32[4,32,8,1]{3,1,0,2:T(8,128)S(1)}, u32[]{:S(2)}, u32[]{:S(2)}) %collective-permute-start.16) | collective-permute-done | bytes 4128 | tf_op jit(solution)/shard_map/ppermute | solution.py:19
  209.6 4.3 collective-permute-done.19
  217.4 7.9 %all-to-all-start.1 = ((f32[32,16,128]{2,1,0:T(8,128)}), f32[32,16,128]{2,1,0:T(8,128)S(1)}, u32[]{:S(2)}, u32[]{:S(2)}) async-start(f32[32,16,128]{2,1,0:T(8,128)} %bitcast.2), calls=%async_computation.1 | async-start | bytes 524288 | tf_op jit(solution)/shard_map/all_to_all | solution.py:103
  228.2 8.4 %all-to-all-done.1 = f32[32,16,128]{2,1,0:T(8,128)S(1)} async-done(((f32[32,16,128]{2,1,0:T(8,128)}), f32[32,16,128]{2,1,0:T(8,128)S(1)}, u32[]{:S(2)}, u32[]{:S(2)}) %all-to-all-start.1) | async-done | bytes 262176 | tf_op jit(solution)/shard_map/all_to_all | solution.py:103
  238.4 3.7 all-to-all-start.3
  248.3 3.4 collective-permute-start.22
  268.2 8.0 %collective-permute-done.20 = f32[4,32,8,1]{3,2,1,0:T(8,128)} collective-permute-done((f32[4,32,8,1]{3,2,1,0:T(8,128)S(1)}, f32[4,32,8,1]{3,2,1,0:T(8,128)}, u32[]{:S(2)}, u32[]{:S(2)}) %collective-permute-start.20) | collective-permute-done | bytes 4128 | tf_op jit(solution)/shard_map/ppermute | solution.py:20
  276.2 12.1 %collective-permute-done.21 = f32[4,32,8,1]{3,2,1,0:T(8,128)} collective-permute-done((f32[4,32,8,1]{3,2,1,0:T(8,128)S(1)}, f32[4,32,8,1]{3,2,1,0:T(8,128)}, u32[]{:S(2)}, u32[]{:S(2)}) %collective-permute-start.21) | collective-permute-done | bytes 4128 | tf_op jit(solution)/shard_map/ppermute | solution.py:19
  296.2 8.8 %collective-permute-start.29 = (f32[2,4,32,128]{3,2,1,0:T(8,128)S(1)}, f32[2,4,32,128]{3,2,1,0:T(8,128)S(1)}, u32[]{:S(2)}, u32[]{:S(2)}) collective-permute-start(f32[2,4,32,128]{3,2,1,0:T(8,128)S(1)} %pad_maximum_fusion.29), channel_id=1, source_target_pairs={{0,384},{32,416},{64,448},{96,480},{128,512},{160,544},{192,576},{... | collective-permute-start | bytes 393224 | tf_op jit(solution)/shard_map/ppermute | solution.py:27
  317.4 8.4 %collective-permute-done.25 = f32[4,32,8,1]{3,2,1,0:T(8,128)} collective-permute-done((f32[4,32,8,1]{3,2,1,0:T(8,128)S(1)}, f32[4,32,8,1]{3,2,1,0:T(8,128)}, u32[]{:S(2)}, u32[]{:S(2)}) %collective-permute-start.25) | collective-permute-done | bytes 4128 | tf_op jit(solution)/shard_map/ppermute | solution.py:20
  325.8 14.1 %collective-permute-done.26 = f32[4,32,8,1]{3,2,1,0:T(8,128)} collective-permute-done((f32[4,32,8,1]{3,2,1,0:T(8,128)S(1)}, f32[4,32,8,1]{3,2,1,0:T(8,128)}, u32[]{:S(2)}, u32[]{:S(2)}) %collective-permute-start.26) | collective-permute-done | bytes 4128 | tf_op jit(solution)/shard_map/ppermute | solution.py:19
  344.0 3.6 collective-permute-start.32
  350.1 3.6 collective-permute-start.30
  357.1 3.7 collective-permute-done.34
  366.5 7.8 %collective-permute-done.30 = f32[4,32,8,1]{3,2,1,0:T(8,128)} collective-permute-done((f32[4,32,8,1]{3,2,1,0:T(8,128)S(1)}, f32[4,32,8,1]{3,2,1,0:T(8,128)}, u32[]{:S(2)}, u32[]{:S(2)}) %collective-permute-start.30) | collective-permute-done | bytes 4128 | tf_op jit(solution)/shard_map/ppermute | solution.py:20
  374.3 11.7 %collective-permute-done.31 = f32[4,32,8,1]{3,2,1,0:T(8,128)} collective-permute-done((f32[4,32,8,1]{3,2,1,0:T(8,128)S(1)}, f32[4,32,8,1]{3,2,1,0:T(8,128)}, u32[]{:S(2)}, u32[]{:S(2)}) %collective-permute-start.31) | collective-permute-done | bytes 4128 | tf_op jit(solution)/shard_map/ppermute | solution.py:19
  390.4 3.5 collective-permute-start.37
  394.6 6.8 %collective-permute-start.39 = (f32[2,4,32,128]{3,2,1,0:T(8,128)}, f32[2,4,32,128]{3,2,1,0:T(8,128)}, u32[]{:S(2)}, u32[]{:S(2)}) collective-permute-start(f32[2,4,32,128]{3,2,1,0:T(8,128)} %pad_maximum_fusion.31), channel_id=1, source_target_pairs={{0,384},{32,416},{64,448},{96,480},{128,512},{160,544},{192,576},{... | collective-permute-start | bytes 393224 | tf_op jit(solution)/shard_map/ppermute | solution.py:27
  412.3 13.3 %collective-permute-done.35 = f32[4,32,8,1]{3,2,1,0:T(8,128)} collective-permute-done((f32[4,32,8,1]{3,2,1,0:T(8,128)}, f32[4,32,8,1]{3,2,1,0:T(8,128)}, u32[]{:S(2)}, u32[]{:S(2)}) %collective-permute-start.35) | collective-permute-done | bytes 4128 | tf_op jit(solution)/shard_map/ppermute | solution.py:20
  425.6 10.3 %collective-permute-done.36 = f32[4,32,8,1]{3,2,1,0:T(8,128)} collective-permute-done((f32[4,32,8,1]{3,2,1,0:T(8,128)}, f32[4,32,8,1]{3,2,1,0:T(8,128)}, u32[]{:S(2)}, u32[]{:S(2)}) %collective-permute-start.36) | collective-permute-done | bytes 4128 | tf_op jit(solution)/shard_map/ppermute | solution.py:19
  (185 shorter events, 143.7 us)
Async XLA Ops:
  2.8 40.2 %all-to-all-start = ((s32[32,16,1]{1,2,0:T(1,128)}), s32[32,16,1]{1,2,0:T(1,128)S(1)}, u32[]{:S(2)}, u32[]{:S(2)}) async-start(s32[32,16,1]{1,2,0:T(1,128)} %bitcast), calls=%async_computation | async-start | bytes 32768 | tf_op jit(solution)/shard_map/all_to_all | solution.py:104
  18.9 35.0 %collective-permute-start.3 = (f32[4,32,1,128]{3,1,0,2:T(8,128)S(1)}, f32[4,32,1,128]{3,1,0,2:T(8,128)S(1)}, u32[]{:S(2)}, u32[]{:S(2)}) collective-permute-start(f32[4,32,1,128]{3,1,0,2:T(8,128)S(1)} %get-tuple-element.250), channel_id=1, source_target_pairs={{1,0},{2,1},{3,2},{4,3},{5,4},{6,5},{7,6},{8,7},{9,8},{10,9},{11,1... | collective-permute-start | bytes 196616 | tf_op jit(solution)/shard_map/ppermute | solution.py:20
  21.1 32.7 %collective-permute-start.2 = (f32[4,32,1,128]{3,1,0,2:T(8,128)S(1)}, f32[4,32,1,128]{3,1,0,2:T(8,128)S(1)}, u32[]{:S(2)}, u32[]{:S(2)}) collective-permute-start(f32[4,32,1,128]{3,1,0,2:T(8,128)S(1)} %get-tuple-element.251), channel_id=1, source_target_pairs={{0,1},{1,2},{2,3},{3,4},{4,5},{5,6},{6,7},{7,8},{8,9},{9,10},{10,1... | collective-permute-start | bytes 196616 | tf_op jit(solution)/shard_map/ppermute | solution.py:19
  24.4 29.4 %collective-permute-start.4 = (f32[2,4,32,128]{3,2,1,0:T(8,128)S(1)}, f32[2,4,32,128]{3,2,1,0:T(8,128)}, u32[]{:S(2)}, u32[]{:S(2)}) collective-permute-start(f32[2,4,32,128]{3,2,1,0:T(8,128)S(1)} %pad_maximum_fusion.24), channel_id=1, source_target_pairs={{0,384},{32,416},{64,448},{96,480},{128,512},{160,544},{192,576},{... | collective-permute-start | bytes 393224 | tf_op jit(solution)/shard_map/ppermute | solution.py:27
  26.6 35.7 %collective-permute-start = (f32[4,32,8,1]{3,1,0,2:T(8,128)S(1)}, f32[4,32,8,1]{3,1,0,2:T(8,128)}, u32[]{:S(2)}, u32[]{:S(2)}) collective-permute-start(f32[4,32,8,1]{3,1,0,2:T(8,128)S(1)} %get-tuple-element.244), channel_id=1, source_target_pairs={{32,0},{64,32},{96,64},{128,96},{160,128},{192,160},{224,192},{256... | collective-permute-start | bytes 12296 | tf_op jit(solution)/shard_map/ppermute | solution.py:20
  41.0 34.0 %collective-permute-start.1 = (f32[4,32,8,1]{3,1,0,2:T(8,128)S(1)}, f32[4,32,8,1]{3,1,0,2:T(8,128)}, u32[]{:S(2)}, u32[]{:S(2)}) collective-permute-start(f32[4,32,8,1]{3,1,0,2:T(8,128)S(1)} %get-tuple-element.245), channel_id=1, source_target_pairs={{0,32},{32,64},{64,96},{96,128},{128,160},{160,192},{192,224},{224... | collective-permute-start | bytes 12296 | tf_op jit(solution)/shard_map/ppermute | solution.py:19
  42.9 174.4 %all-to-all-start.2 = ((f32[32,16,128]{2,1,0:T(8,128)}), f32[32,16,128]{2,1,0:T(8,128)S(1)}, u32[]{:S(2)}, u32[]{:S(2)}) async-start(f32[32,16,128]{2,1,0:T(8,128)} %bitcast.4), calls=%async_computation.2 | async-start | bytes 524288 | tf_op jit(solution)/shard_map/all_to_all | solution.py:102
  76.7 15.9 %collective-permute-start.8 = (f32[4,32,1,128]{3,1,0,2:T(8,128)S(1)}, f32[4,32,1,128]{3,1,0,2:T(8,128)S(1)}, u32[]{:S(2)}, u32[]{:S(2)}) collective-permute-start(f32[4,32,1,128]{3,1,0,2:T(8,128)S(1)} %get-tuple-element.242), channel_id=1, source_target_pairs={{1,0},{2,1},{3,2},{4,3},{5,4},{6,5},{7,6},{8,7},{9,8},{10,9},{11,1... | collective-permute-start | bytes 196616 | tf_op jit(solution)/shard_map/ppermute | solution.py:20
  87.3 23.0 %collective-permute-start.5 = (f32[4,32,8,1]{3,1,0,2:T(8,128)S(1)}, f32[4,32,8,1]{3,1,0,2:T(8,128)S(1)}, u32[]{:S(2)}, u32[]{:S(2)}) collective-permute-start(f32[4,32,8,1]{3,1,0,2:T(8,128)S(1)} %get-tuple-element.238), channel_id=1, source_target_pairs={{32,0},{64,32},{96,64},{128,96},{160,128},{192,160},{224,192},{256... | collective-permute-start | bytes 12296 | tf_op jit(solution)/shard_map/ppermute | solution.py:20
  89.2 31.0 %collective-permute-start.6 = (f32[4,32,8,1]{3,1,0,2:T(8,128)S(1)}, f32[4,32,8,1]{3,1,0,2:T(8,128)S(1)}, u32[]{:S(2)}, u32[]{:S(2)}) collective-permute-start(f32[4,32,8,1]{3,1,0,2:T(8,128)S(1)} %get-tuple-element.239), channel_id=1, source_target_pairs={{0,32},{32,64},{64,96},{96,128},{128,160},{160,192},{192,224},{224... | collective-permute-start | bytes 12296 | tf_op jit(solution)/shard_map/ppermute | solution.py:19
  120.9 17.0 %collective-permute-start.13 = (f32[4,32,1,128]{3,1,0,2:T(8,128)S(1)}, f32[4,32,1,128]{3,1,0,2:T(8,128)S(1)}, u32[]{:S(2)}, u32[]{:S(2)}) collective-permute-start(f32[4,32,1,128]{3,1,0,2:T(8,128)S(1)} %get-tuple-element.236), channel_id=1, source_target_pairs={{1,0},{2,1},{3,2},{4,3},{5,4},{6,5},{7,6},{8,7},{9,8},{10,9},{11,1... | collective-permute-start | bytes 196616 | tf_op jit(solution)/shard_map/ppermute | solution.py:20
  132.6 22.5 %collective-permute-start.10 = (f32[4,32,8,1]{3,1,0,2:T(8,128)S(1)}, f32[4,32,8,1]{3,1,0,2:T(8,128)S(1)}, u32[]{:S(2)}, u32[]{:S(2)}) collective-permute-start(f32[4,32,8,1]{3,1,0,2:T(8,128)S(1)} %get-tuple-element.232), channel_id=1, source_target_pairs={{32,0},{64,32},{96,64},{128,96},{160,128},{192,160},{224,192},{256... | collective-permute-start | bytes 12296 | tf_op jit(solution)/shard_map/ppermute | solution.py:20
  134.5 33.0 %collective-permute-start.11 = (f32[4,32,8,1]{3,1,0,2:T(8,128)S(1)}, f32[4,32,8,1]{3,1,0,2:T(8,128)S(1)}, u32[]{:S(2)}, u32[]{:S(2)}) collective-permute-start(f32[4,32,8,1]{3,1,0,2:T(8,128)S(1)} %get-tuple-element.233), channel_id=1, source_target_pairs={{0,32},{32,64},{64,96},{96,128},{128,160},{160,192},{192,224},{224... | collective-permute-start | bytes 12296 | tf_op jit(solution)/shard_map/ppermute | solution.py:19
  168.5 40.9 %collective-permute-start.17 = (f32[4,32,1,128]{3,1,0,2:T(8,128)S(1)}, f32[4,32,1,128]{3,1,0,2:T(8,128)S(1)}, u32[]{:S(2)}, u32[]{:S(2)}) collective-permute-start(f32[4,32,1,128]{3,1,0,2:T(8,128)S(1)} %bitcast.204), channel_id=1, source_target_pairs={{0,1},{1,2},{2,3},{3,4},{4,5},{5,6},{6,7},{7,8},{8,9},{9,10},{10,1... | collective-permute-start | bytes 196616 | tf_op jit(solution)/shard_map/ppermute | solution.py:19
  170.4 39.0 %collective-permute-start.18 = (f32[4,32,1,128]{3,2,1,0:T(1,128)S(1)}, f32[4,32,1,128]{3,2,1,0:T(1,128)S(1)}, u32[]{:S(2)}, u32[]{:S(2)}) collective-permute-start(f32[4,32,1,128]{3,2,1,0:T(1,128)S(1)} %get-tuple-element.231), channel_id=1, source_target_pairs={{1,0},{2,1},{3,2},{4,3},{5,4},{6,5},{7,6},{8,7},{9,8},{10,9},{11,1... | collective-permute-start | bytes 196616 | tf_op jit(solution)/shard_map/ppermute | solution.py:20
  173.0 24.3 %collective-permute-start.15 = (f32[4,32,8,1]{3,1,0,2:T(8,128)S(1)}, f32[4,32,8,1]{3,1,0,2:T(8,128)S(1)}, u32[]{:S(2)}, u32[]{:S(2)}) collective-permute-start(f32[4,32,8,1]{3,1,0,2:T(8,128)S(1)} %get-tuple-element.228), channel_id=1, source_target_pairs={{32,0},{64,32},{96,64},{128,96},{160,128},{192,160},{224,192},{256... | collective-permute-start | bytes 12296 | tf_op jit(solution)/shard_map/ppermute | solution.py:20
  175.0 33.9 %collective-permute-start.16 = (f32[4,32,8,1]{3,1,0,2:T(8,128)S(1)}, f32[4,32,8,1]{3,1,0,2:T(8,128)S(1)}, u32[]{:S(2)}, u32[]{:S(2)}) collective-permute-start(f32[4,32,8,1]{3,1,0,2:T(8,128)S(1)} %get-tuple-element.229), channel_id=1, source_target_pairs={{0,32},{32,64},{64,96},{96,128},{128,160},{160,192},{192,224},{224... | collective-permute-start | bytes 12296 | tf_op jit(solution)/shard_map/ppermute | solution.py:19
  178.4 35.5 %collective-permute-start.19 = (f32[2,4,32,128]{3,2,1,0:T(8,128)S(1)}, f32[2,4,32,128]{3,2,1,0:T(8,128)S(1)}, u32[]{:S(2)}, u32[]{:S(2)}) collective-permute-start(f32[2,4,32,128]{3,2,1,0:T(8,128)S(1)} %pad_maximum_fusion.27), channel_id=1, source_target_pairs={{0,384},{32,416},{64,448},{96,480},{128,512},{160,544},{192,576},{... | collective-permute-start | bytes 393224 | tf_op jit(solution)/shard_map/ppermute | solution.py:27
  217.4 19.2 %all-to-all-start.1 = ((f32[32,16,128]{2,1,0:T(8,128)}), f32[32,16,128]{2,1,0:T(8,128)S(1)}, u32[]{:S(2)}, u32[]{:S(2)}) async-start(f32[32,16,128]{2,1,0:T(8,128)} %bitcast.2), calls=%async_computation.1 | async-start | bytes 524288 | tf_op jit(solution)/shard_map/all_to_all | solution.py:103
  238.4 170.2 %all-to-all-start.3 = ((f32[32,16,128]{2,1,0:T(8,128)}), f32[32,16,128]{2,1,0:T(8,128)S(1)}, u32[]{:S(2)}, u32[]{:S(2)}) async-start(f32[32,16,128]{2,1,0:T(8,128)} %bitcast.60), calls=%async_computation.3 | async-start | bytes 524288 | tf_op jit(solution)/shard_map/all_to_all | solution.py:114
  254.1 22.1 %collective-permute-start.20 = (f32[4,32,8,1]{3,2,1,0:T(8,128)S(1)}, f32[4,32,8,1]{3,2,1,0:T(8,128)}, u32[]{:S(2)}, u32[]{:S(2)}) collective-permute-start(f32[4,32,8,1]{3,2,1,0:T(8,128)S(1)} %get-tuple-element.222), channel_id=1, source_target_pairs={{32,0},{64,32},{96,64},{128,96},{160,128},{192,160},{224,192},{256... | collective-permute-start | bytes 12296 | tf_op jit(solution)/shard_map/ppermute | solution.py:20
  256.0 32.2 %collective-permute-start.21 = (f32[4,32,8,1]{3,2,1,0:T(8,128)S(1)}, f32[4,32,8,1]{3,2,1,0:T(8,128)}, u32[]{:S(2)}, u32[]{:S(2)}) collective-permute-start(f32[4,32,8,1]{3,2,1,0:T(8,128)S(1)} %get-tuple-element.223), channel_id=1, source_target_pairs={{0,32},{32,64},{64,96},{96,128},{128,160},{160,192},{192,224},{224... | collective-permute-start | bytes 12296 | tf_op jit(solution)/shard_map/ppermute | solution.py:19
  290.6 19.9 %collective-permute-start.28 = (f32[4,32,1,128]{3,1,0,2:T(8,128)S(1)}, f32[4,32,1,128]{3,1,0,2:T(8,128)S(1)}, u32[]{:S(2)}, u32[]{:S(2)}) collective-permute-start(f32[4,32,1,128]{3,1,0,2:T(8,128)S(1)} %bitcast.216), channel_id=1, source_target_pairs={{1,0},{2,1},{3,2},{4,3},{5,4},{6,5},{7,6},{8,7},{9,8},{10,9},{11,1... | collective-permute-start | bytes 196616 | tf_op jit(solution)/shard_map/ppermute | solution.py:20
  292.8 17.7 %collective-permute-start.27 = (f32[4,32,1,128]{3,1,0,2:T(8,128)S(1)}, f32[4,32,1,128]{3,1,0,2:T(8,128)S(1)}, u32[]{:S(2)}, u32[]{:S(2)}) collective-permute-start(f32[4,32,1,128]{3,1,0,2:T(8,128)S(1)} %bitcast.208), channel_id=1, source_target_pairs={{0,1},{1,2},{2,3},{3,4},{4,5},{5,6},{6,7},{7,8},{8,9},{9,10},{10,1... | collective-permute-start | bytes 196616 | tf_op jit(solution)/shard_map/ppermute | solution.py:19
  305.1 20.6 %collective-permute-start.25 = (f32[4,32,8,1]{3,2,1,0:T(8,128)S(1)}, f32[4,32,8,1]{3,2,1,0:T(8,128)}, u32[]{:S(2)}, u32[]{:S(2)}) collective-permute-start(f32[4,32,8,1]{3,2,1,0:T(8,128)S(1)} %get-tuple-element.218), channel_id=1, source_target_pairs={{32,0},{64,32},{96,64},{128,96},{160,128},{192,160},{224,192},{256... | collective-permute-start | bytes 12296 | tf_op jit(solution)/shard_map/ppermute | solution.py:20
  307.1 32.8 %collective-permute-start.26 = (f32[4,32,8,1]{3,2,1,0:T(8,128)S(1)}, f32[4,32,8,1]{3,2,1,0:T(8,128)}, u32[]{:S(2)}, u32[]{:S(2)}) collective-permute-start(f32[4,32,8,1]{3,2,1,0:T(8,128)S(1)} %get-tuple-element.219), channel_id=1, source_target_pairs={{0,32},{32,64},{64,96},{96,128},{128,160},{160,192},{192,224},{224... | collective-permute-start | bytes 12296 | tf_op jit(solution)/shard_map/ppermute | solution.py:19
  350.1 24.2 %collective-permute-start.30 = (f32[4,32,8,1]{3,2,1,0:T(8,128)S(1)}, f32[4,32,8,1]{3,2,1,0:T(8,128)}, u32[]{:S(2)}, u32[]{:S(2)}) collective-permute-start(f32[4,32,8,1]{3,2,1,0:T(8,128)S(1)} %get-tuple-element.214), channel_id=1, source_target_pairs={{32,0},{64,32},{96,64},{128,96},{160,128},{192,160},{224,192},{256... | collective-permute-start | bytes 12296 | tf_op jit(solution)/shard_map/ppermute | solution.py:20
  353.8 32.3 %collective-permute-start.31 = (f32[4,32,8,1]{3,2,1,0:T(8,128)S(1)}, f32[4,32,8,1]{3,2,1,0:T(8,128)}, u32[]{:S(2)}, u32[]{:S(2)}) collective-permute-start(f32[4,32,8,1]{3,2,1,0:T(8,128)S(1)} %get-tuple-element.215), channel_id=1, source_target_pairs={{0,32},{32,64},{64,96},{96,128},{128,160},{160,192},{192,224},{224... | collective-permute-start | bytes 12296 | tf_op jit(solution)/shard_map/ppermute | solution.py:19
  388.3 19.4 %collective-permute-start.38 = (f32[4,32,1,128]{3,1,0,2:T(8,128)S(1)}, f32[4,32,1,128]{3,1,0,2:T(8,128)S(1)}, u32[]{:S(2)}, u32[]{:S(2)}) collective-permute-start(f32[4,32,1,128]{3,1,0,2:T(8,128)S(1)} %bitcast.220), channel_id=1, source_target_pairs={{1,0},{2,1},{3,2},{4,3},{5,4},{6,5},{7,6},{8,7},{9,8},{10,9},{11,1... | collective-permute-start | bytes 196616 | tf_op jit(solution)/shard_map/ppermute | solution.py:20
  390.4 17.3 %collective-permute-start.37 = (f32[4,32,1,128]{3,1,0,2:T(8,128)S(1)}, f32[4,32,1,128]{3,1,0,2:T(8,128)S(1)}, u32[]{:S(2)}, u32[]{:S(2)}) collective-permute-start(f32[4,32,1,128]{3,1,0,2:T(8,128)S(1)} %bitcast.212), channel_id=1, source_target_pairs={{0,1},{1,2},{2,3},{3,4},{4,5},{5,6},{6,7},{7,8},{8,9},{9,10},{10,1... | collective-permute-start | bytes 196616 | tf_op jit(solution)/shard_map/ppermute | solution.py:19
  402.5 23.1 %collective-permute-start.35 = (f32[4,32,8,1]{3,2,1,0:T(8,128)}, f32[4,32,8,1]{3,2,1,0:T(8,128)}, u32[]{:S(2)}, u32[]{:S(2)}) collective-permute-start(f32[4,32,8,1]{3,2,1,0:T(8,128)} %get-tuple-element.210), channel_id=1, source_target_pairs={{32,0},{64,32},{96,64},{128,96},{160,128},{192,160},{224,192},{256... | collective-permute-start | bytes 12296 | tf_op jit(solution)/shard_map/ppermute | solution.py:20
  404.4 31.5 %collective-permute-start.36 = (f32[4,32,8,1]{3,2,1,0:T(8,128)}, f32[4,32,8,1]{3,2,1,0:T(8,128)}, u32[]{:S(2)}, u32[]{:S(2)}) collective-permute-start(f32[4,32,8,1]{3,2,1,0:T(8,128)} %get-tuple-element.211), channel_id=1, source_target_pairs={{0,32},{32,64},{64,96},{96,128},{128,160},{160,192},{192,224},{224... | collective-permute-start | bytes 12296 | tf_op jit(solution)/shard_map/ppermute | solution.py:19
  (23 other events, 197.7 us)
where the time goes:
time: 443 us; the launch traced here: 439 us
  waiting for transfers between devices  208 us (47%)
  starting transfers between devices  169 us (38%)
  local copies, waits for them, and re-layouts  32.5 us (7%)
  other arithmetic  25.7 us (6%)
    ppermute x16, waiting for transfers between devices, with_halo(): before = lax.ppermute(last, axis, up)  94.8 us
    ppermute x16, waiting for transfers between devices, with_halo(): after = lax.ppermute(first, axis, down)  91.8 us
    ppermute x16, starting transfers between devices, with_halo(): before = lax.ppermute(last, axis, up)  48.6 us
    ppermute x16, starting transfers between devices, with_halo(): after = lax.ppermute(first, axis, down)  48.4 us
    ppermute x8, starting transfers between devices, from_behind(): lax.ppermute(shard, axis, [(i, (i + by) % peers) for i in range(peers)])  35.7 us
    scatter x10, local copies, waits for them, and re-layouts, spread_once(): padded_lat.at[:, :, 0, :].set(south_rim).at[:, :, -1, :].set(north_rim)  22.1 us
    all_to_all x1, starting transfers between devices, local(): lax.all_to_all(slot_code, 'lat', split_axis=0, concat_axis=0, tiled=True)  14.1 us
    ppermute x8, waiting for transfers between devices, from_behind(): lax.ppermute(shard, axis, [(i, (i + by) % peers) for i in range(peers)])  12.6 us
  transfers between devices with their start and end apart: 44, of which 21 were waited for; matrix products, arithmetic and copies ran while one was open for 12% of the time, Pallas kernels for 0%

commit v1 on v0

v1 whole, which is shorter than its diff:
```python
import functools

import jax
import jax.numpy as jnp
from jax import lax
from jax.experimental import pallas as pl
from jax.experimental.pallas import tpu as pltpu
from jax.sharding import PartitionSpec as P

HALO = 4
STEPS = 4
ROWS = 8
EXT = ROWS + 2 * HALO
LANES = 128
FIELDS = 4
PROFILE = 128
GROUPS = PROFILE // 8
KINDS = 3
F32 = jnp.float32
BF16 = jnp.bfloat16


def lane_iota(shape):
    return lax.broadcasted_iota(jnp.int32, shape, len(shape) - 1)


def split(x):
    hi = x.astype(BF16)
    return hi, (x - hi.astype(F32)).astype(BF16)


def kernel(
    n_lon, n_lat, slots,
    inc_h, clon_h, clat_h, obs_h, wgt_h, op_h, col_h, typ_h, cnt_h,
    grad_o, dep_o,
    inc_v, cf_v, op_v, col_v, typ_v, cnt_v, obs_v, wgt_v, code_v, codes_in, codet_v, dep_v, out_v,
    xa, pa, xe, pe, coefs, strips, edges, state_v, st_v, oh_v, opf_v, opb_v, lhs_hi, lhs_lo, adj_v,
    load_sem, own_sem, send_sem, recv_row, recv_corner, recv_side, a2a_send, a2a_recv,
):
    lon, lat = lax.axis_index("lon"), lax.axis_index("lat")
    n_rows = n_lat * slots
    tiles = n_rows // LANES
    per_tile = LANES // slots
    south, north = lat == 0, lat == n_lat - 1
    south_i, north_i = south.astype(jnp.int32), north.astype(jnp.int32)
    opposite = n_lon // 2

    def lon_at(by):
        return lax.rem(lon + by + n_lon, n_lon)

    def prev_of(d):
        return (lon_at(d + opposite * south_i), lat - 1 + south_i)

    def next_of(d):
        return (lon_at(d + opposite * north_i), lat + 1 - north_i)

    def dev(where):
        return {"lon": where[0], "lat": where[1]}

    barrier = pltpu.get_barrier_semaphore()

    def greet(where):
        pl.semaphore_signal(barrier, inc=1, device_id=dev(where), device_id_type=pl.DeviceIdType.MESH)

    for d in (-1, 1):
        greet(prev_of(d))
        greet(next_of(d))
        greet((lon_at(d), lat))

    @pl.when(south)
    def _():
        greet(prev_of(0))

    @pl.when(north)
    def _():
        greet(next_of(0))

    @pl.loop(1, n_lat)
    def _(k):
        greet((lon, lax.rem(lat + k, n_lat)))

    loads = [
        pltpu.make_async_copy(src, dst, load_sem.at[i])
        for i, (src, dst) in enumerate(
            (
                (inc_h, inc_v), (clon_h, cf_v.at[0]), (clat_h, cf_v.at[1]), (op_h, op_v),
                (col_h, col_v), (typ_h, typ_v), (cnt_h, cnt_v),
            )
        )
    ]
    for load in loads:
        load.start()
    mine = pl.ds(pl.multiple_of(lat * slots, slots), slots)
    own = [
        pltpu.make_async_copy(obs_h.at[mine], obs_v.at[mine], own_sem.at[0]),
        pltpu.make_async_copy(wgt_h.at[mine], wgt_v.at[mine], own_sem.at[1]),
    ]
    for copy in own:
        copy.start()
    lane = lane_iota((8, LANES))
    slot_of = lane >> 3
    in_slot = lane & 7

    for i in (4, 5, 6):
        loads[i].wait()
    rep = (lane_iota((n_lat, n_rows)) // slots == lax.broadcasted_iota(jnp.int32, (n_lat, n_rows), 0)).astype(F32).astype(BF16)
    counts = jnp.broadcast_to(cnt_v[...].astype(F32), (8, n_lat)).astype(BF16)
    limit = jnp.dot(counts, rep, preferred_element_type=F32)
    for q in range(tiles):
        lim = limit[0:1, q * LANES : (q + 1) * LANES].astype(jnp.int32)
        code = col_v[q : q + 1, :] * 4 + typ_v[q : q + 1, :] + 1
        code_v[q] = jnp.where(lane_iota((1, LANES)) % slots < lim, code, 0)

    def pack(v):
        packed = jnp.zeros((8, LANES), F32)
        for s in range(GROUPS):
            packed = jnp.where(slot_of == s, pltpu.roll(v(s), 8 * s + HALO, 1), packed)
        return packed

    for i in (0, 1, 2):
        loads[i].wait()

    @pl.loop(0, ROWS)
    def _(r):
        for s in range(GROUPS):
            xa[r + HALO, s * 8 : (s + 1) * 8, :] = inc_v[pl.ds(s * 64 + r, 8, stride=8), :]
        for ct in range(2):
            xa[r + HALO, PROFILE + ct * 4 : PROFILE + ct * 4 + 4, :] = cf_v[ct, pl.ds(r, 4, stride=8), :]
        pa[1, r + HALO, 0:8, :] = pack(lambda s: xa[r + HALO, s * 8 : (s + 1) * 8, :])
        both = xa[r + HALO, PROFILE : PROFILE + 8, :]
        table = pack(lambda s: both)
        for ct in range(2):
            coef = jnp.zeros((8, LANES), F32)
            for f in range(FIELDS):
                coef = jnp.where(slot_of >> 2 == f, jnp.broadcast_to(table[ct * 4 + f : ct * 4 + f + 1, :], (8, LANES)), coef)
            pa[1, r + HALO, 8 + ct * 8 : 16 + ct * 8, :] = coef

    def expand(r):
        for f in range(FIELDS):
            a = jnp.broadcast_to(xa[r, PROFILE + f : PROFILE + f + 1, :], (8, LANES))
            b = jnp.broadcast_to(xa[r, PROFILE + 4 + f : PROFILE + 5 + f, :], (8, LANES))
            coefs[0, r, f] = a
            coefs[1, r, f] = b
            coefs[2, r, f] = 1.0 - 2.0 * (a * a + b * b)

    pl.semaphore_wait(barrier, n_lat - 1 + 6 + south_i + north_i)

    low, high = pl.ds(HALO, HALO), pl.ds(2 * HALO, HALO)
    to_prev = pl.ds(3 * HALO * (1 - south_i), HALO)
    to_next = pl.ds(3 * HALO * north_i, HALO)
    prev_side, next_side = 1 - south_i, north_i

    def exchange(phase, x, p):
        def send(i, src, dst, sem, where):
            return pltpu.make_async_remote_copy(
                src_ref=src, dst_ref=dst, send_sem=send_sem.at[phase, i], recv_sem=sem,
                device_id=dev(where), device_id_type=pl.DeviceIdType.MESH,
            )

        copies = [
            send(0, x.at[low], x.at[to_prev], recv_row.at[phase, prev_side], prev_of(0)),
            send(1, x.at[high], x.at[to_next], recv_row.at[phase, next_side], next_of(0)),
        ]
        own_rows = pl.ds(HALO, ROWS)
        for i, d in enumerate((-1, 1)):
            copies.append(send(2 + i, p.at[1, own_rows], p.at[1 - d, own_rows], recv_side.at[phase, i], (lon_at(d), lat)))
        for i, d in enumerate((-1, 0, 1)):
            copies.append(send(4 + i, p.at[1, low], p.at[1 - d, to_prev], recv_corner.at[phase, prev_side, i], prev_of(d)))
            copies.append(send(7 + i, p.at[1, high], p.at[1 - d, to_next], recv_corner.at[phase, next_side, i], next_of(d)))
        return copies

    def settle(phase, x, p):
        def arrive(ref, sem):
            pltpu.make_async_copy(ref, ref, sem).wait()

        own_rows = pl.ds(HALO, ROWS)
        for i, d in enumerate((-1, 1)):
            arrive(p.at[1 - d, own_rows], recv_side.at[phase, i])
        for side, rows in enumerate((pl.ds(0, HALO), pl.ds(3 * HALO, HALO))):
            for i, d in enumerate((-1, 0, 1)):
                arrive(p.at[1 - d, rows], recv_corner.at[phase, side, i])
            arrive(x.at[rows], recv_row.at[phase, side])

    first = exchange(0, xa, pa)
    for copy in first:
        copy.start()

    @pl.loop(1, n_lat)
    def _(k):
        to = lax.rem(lat + k, n_lat)
        pltpu.make_async_remote_copy(
            src_ref=code_v.at[to // per_tile], dst_ref=codes_in.at[lat], send_sem=a2a_send.at[0], recv_sem=a2a_recv.at[0],
            device_id=dev((lon, to)), device_id_type=pl.DeviceIdType.MESH,
        ).start()

    @pl.loop(1, n_lat)
    def _(k):
        to = lax.rem(lat + k, n_lat)
        theirs = pl.ds(pl.multiple_of(to * slots, slots), slots)
        for i, (src, dst) in enumerate(((obs_h, obs_v), (wgt_h, wgt_v))):
            pltpu.make_async_remote_copy(
                src_ref=src.at[theirs], dst_ref=dst.at[mine], send_sem=a2a_send.at[1 + i], recv_sem=a2a_recv.at[1 + i],
                device_id=dev((lon, to)), device_id_type=pl.DeviceIdType.MESH,
            ).start()

    def all_but_one(ref, sem):
        part = ref.at[pl.ds(0, ref.shape[0] // n_lat * (n_lat - 1))]
        pltpu.make_async_copy(part, part, sem).wait()

    loads[3].wait()
    for k in range(KINDS):
        hi, lo = split(op_v[k])
        opf_v[k * PROFILE : (k + 1) * PROFILE, :] = jnp.concatenate([hi, lo], 1)
        hi, lo = split(jnp.transpose(op_v[k]))
        opb_v[k * PROFILE : (k + 1) * PROFILE, :] = jnp.concatenate([hi, lo], 1)

    @pl.loop(HALO, HALO + ROWS)
    def _(r):
        expand(r)

    all_but_one(codes_in, a2a_recv.at[0])
    codes_in[lat] = code_v[lat // per_tile]
    mod = lax.rem(lat, per_tile)
    lane_1 = lane_iota((1, LANES))
    for q in range(tiles):
        row = jnp.zeros((1, LANES), jnp.int32)
        for j in range(per_tile):
            moved = pltpu.roll(codes_in[q * per_tile + j], lax.rem(LANES + slots * (j - mod), LANES), 1)
            row = jnp.where(lane_1 // slots == j, moved, row)
        turned = jnp.transpose(jnp.broadcast_to(row.astype(F32), (LANES, LANES))).astype(jnp.int32)
        codet_v[q * LANES : (q + 1) * LANES, :] = turned
        cell = (turned - 1) >> 2
        for r in range(ROWS):
            hit = cell == lane_iota((LANES, LANES)) + r * LANES
            oh_v[q * LANES : (q + 1) * LANES, r * LANES : (r + 1) * LANES] = jnp.where(hit, 1.0, 0.0).astype(BF16)

    sign_south = jnp.where(south, -1.0, 1.0).astype(F32)
    sign_north = jnp.where(north, -1.0, 1.0).astype(F32)
    def row_at(r):
        if r < HALO:
            return r + (HALO - 1 - 2 * r) * south_i
        if r >= HALO + ROWS:
            j = r - HALO - ROWS
            return r + (HALO - 1 - 2 * j) * north_i
        return r

    def sign_at(r):
        return sign_south if r < HALO else sign_north if r >= HALO + ROWS else None

    def merged(p, r, part):
        at = row_at(r)
        rows = slice(part * 8, part * 8 + 8)
        west, mid, east = p[0, at, rows, :], p[1, at, rows, :], p[2, at, rows, :]
        return jnp.where(in_slot < HALO, west, mid), jnp.where(in_slot < HALO, mid, east)

    def evolve_strips(p):
        cur = [[None] * EXT, [None] * EXT]
        for r in range(EXT):
            w, z = merged(p, r, 0)
            if sign_at(r) is not None:
                sign = jnp.where(lane >= 64, sign_at(r), 1.0)
                w, z = w * sign, z * sign
            cur[0][r], cur[1][r] = w, z
        for t in range(STEPS):
            inner = range(t + 1, EXT - 1 - t)
            g = [{}, {}]
            for side in range(2):
                for r in inner:
                    g[side][r] = strips[side, 0, r] * cur[side][r]
            for r in inner:
                edges[t, r] = jnp.where(in_slot == 2, pltpu.roll(g[1][r], LANES - 2, 1), g[0][r])
            if t < STEPS - 1:
                for side in range(2):
                    h = {r: strips[side, 1, r] * cur[side][r] for r in range(t, EXT - t)}
                    new = [None] * EXT
                    for r in inner:
                        gr = g[side][r]
                        new[r] = (
                            strips[side, 2, r] * cur[side][r]
                            + strips[side, 0, r] * (pltpu.roll(gr, 1, 1) + pltpu.roll(gr, LANES - 1, 1))
                            + strips[side, 1, r] * (h[r - 1] + h[r + 1])
                        )
                    cur[side] = new

    def diffuse(x, give):
        @pl.loop(0, GROUPS)
        def _(s):
            f = s // 4
            rows = pl.ds(pl.multiple_of(s * 8, 8), 8)
            wind = s >= GROUPS // 2
            flip_s = jnp.where(wind, sign_south, 1.0)
            flip_n = jnp.where(wind, sign_north, 1.0)
            turn = LANES - HALO + 1 - 8 * s
            cur = []
            for r in range(EXT):
                v = x[row_at(r), rows, :]
                if r < HALO:
                    v = v * flip_s
                if r >= HALO + ROWS:
                    v = v * flip_n
                cur.append(v)
            for t in range(STEPS):
                h = {r: coefs[1, r, f] * cur[r] for r in range(t, EXT - t)}
                new = [None] * EXT
                for r in range(t + 1, EXT - 1 - t):
                    a = coefs[0, r, f]
                    g = a * cur[r]
                    e = pltpu.roll(edges[t, r], turn, 1)
                    lateral = jnp.where(lane == 0, e, pltpu.roll(g, 1, 1)) + jnp.where(lane == LANES - 1, e, pltpu.roll(g, LANES - 1, 1))
                    new[r] = coefs[2, r, f] * cur[r] + a * lateral + coefs[1, r, f] * (h[r - 1] + h[r + 1])
                cur = new
            for r in range(ROWS):
                give(r, s, cur[r + HALO])

    settle(0, xa, pa)
    for r in range(EXT):
        for ct in range(2):
            w, z = merged(pa, r, 1 + ct)
            strips[0, ct, r], strips[1, ct, r] = w, z
        for side in range(2):
            a, b = strips[side, 0, r], strips[side, 1, r]
            strips[side, 2, r] = 1.0 - 2.0 * (a * a + b * b)
    for r in list(range(HALO)) + list(range(HALO + ROWS, EXT)):
        at = row_at(r)
        for f in range(FIELDS):
            a = jnp.broadcast_to(xa[at, PROFILE + f : PROFILE + f + 1, :], (8, LANES))
            b = jnp.broadcast_to(xa[at, PROFILE + 4 + f : PROFILE + 5 + f, :], (8, LANES))
            coefs[0, r, f] = a
            coefs[1, r, f] = b
            coefs[2, r, f] = 1.0 - 2.0 * (a * a + b * b)
    evolve_strips(pa)

    def keep_state(r, s, v):
        state_v[r, pl.ds(pl.multiple_of(s * 8, 8), 8), :] = v

    diffuse(xa, keep_state)

    for r in range(ROWS):
        hi, lo = split(jnp.transpose(state_v[r]))
        st_v[r * LANES : (r + 1) * LANES, :] = jnp.concatenate([hi, lo], 1)
    found = jnp.dot(oh_v[...], st_v[...], preferred_element_type=F32)
    columns = found[:, :PROFILE] + found[:, PROFILE:]

    def by_kind(values, table):
        hi, lo = split(values)
        kind = codet_v[...]
        kind = (kind - 1) & 3
        for k in range(KINDS):
            of_kind = kind == k
            lhs_hi[:, k * PROFILE : (k + 1) * PROFILE] = jnp.where(of_kind, hi.astype(F32), 0.0).astype(BF16)
            lhs_lo[:, k * PROFILE : (k + 1) * PROFILE] = jnp.where(of_kind, lo.astype(F32), 0.0).astype(BF16)
        one = jnp.dot(lhs_hi[...], table[...], preferred_element_type=F32)
        two = jnp.dot(lhs_lo[...], table[:, :PROFILE], preferred_element_type=F32)
        return one[:, :PROFILE] + one[:, PROFILE:] + two

    model = by_kind(columns, opf_v)
    for copy in own:
        copy.wait()
    all_but_one(obs_v, a2a_recv.at[1])
    all_but_one(wgt_v, a2a_recv.at[2])
    dep = jnp.where(codet_v[...] > 0, obs_v[...] - model, 0.0)
    dep_v[...] = dep
    adj = by_kind(wgt_v[...] * dep, opb_v)
    hi, lo = split(jnp.transpose(adj))
    adj_v[0:PROFILE, :] = hi
    adj_v[PROFILE : 2 * PROFILE, :] = lo
    for part in range(2):
        spread = jnp.dot(adj_v[...], oh_v[:, part * 4 * LANES : (part + 1) * 4 * LANES], preferred_element_type=F32)
        for r in range(4):
            xe[HALO + part * 4 + r] = spread[:PROFILE, r * LANES : (r + 1) * LANES] + spread[PROFILE:, r * LANES : (r + 1) * LANES]

    @pl.loop(HALO, HALO + ROWS)
    def _(r):
        pe[1, r] = pack(lambda s: xe[r, s * 8 : (s + 1) * 8, :])

    second = exchange(1, xe, pe)
    for copy in second:
        copy.start()

    back = pltpu.make_async_copy(dep_v.at[mine], dep_o.at[mine], own_sem.at[2])
    back.start()

    @pl.loop(1, n_lat)
    def _(k):
        to = lax.rem(lat + k, n_lat)
        theirs = pl.ds(pl.multiple_of(to * slots, slots), slots)
        pltpu.make_async_remote_copy(
            src_ref=dep_v.at[theirs], dst_ref=dep_o.at[mine], send_sem=a2a_send.at[3], recv_sem=a2a_recv.at[3],
            device_id=dev((lon, to)), device_id_type=pl.DeviceIdType.MESH,
        ).start()

    settle(1, xe, pe)
    evolve_strips(pe)

    def keep_gradient(r, s, v):
        rows = pl.ds(s * 64 + r, 8, stride=8)
        out_v[rows, :] = inc_v[rows, :] - v

    diffuse(xe, keep_gradient)
    last = pltpu.make_async_copy(out_v, grad_o, load_sem.at[0])
    last.start()

    for copy in first + second:
        copy.wait_send()
    all_but_one(codes_in, a2a_send.at[0])
    all_but_one(obs_v, a2a_send.at[1])
    all_but_one(wgt_v, a2a_send.at[2])
    all_but_one(dep_v, a2a_send.at[3])
    all_but_one(dep_o, a2a_recv.at[3])
    back.wait()
    last.wait()


def local(n_lon, n_lat, increment, coef_lon, coef_lat, obs_values, obs_weight, obs_operator, obs_columns, obs_types, obs_counts):
    n_rows = obs_columns.shape[0]
    slots = n_rows // n_lat
    tiles = n_rows // LANES
    cells = ROWS * LANES
    any_spec = pl.BlockSpec(memory_space=pl.ANY)
    gradient, departures = pl.pallas_call(
        functools.partial(kernel, n_lon, n_lat, slots),
        out_shape=(
            jax.ShapeDtypeStruct((PROFILE * ROWS, LANES), F32),
            jax.ShapeDtypeStruct((n_rows, PROFILE), F32),
        ),
        in_specs=[any_spec] * 9,
        out_specs=(any_spec, any_spec),
        scratch_shapes=[
            pltpu.VMEM((PROFILE * ROWS, LANES), F32),
            pltpu.VMEM((2, FIELDS * ROWS, LANES), F32),
            pltpu.VMEM((KINDS, PROFILE, PROFILE), F32),
            pltpu.VMEM((tiles, LANES), jnp.int32),
            pltpu.VMEM((tiles, LANES), jnp.int32),
            pltpu.VMEM((1, n_lat), jnp.int32),
            pltpu.VMEM((n_rows, PROFILE), F32),
            pltpu.VMEM((n_rows, PROFILE), F32),
            pltpu.VMEM((tiles, 1, LANES), jnp.int32),
            pltpu.VMEM((n_lat, 1, LANES), jnp.int32),
            pltpu.VMEM((n_rows, LANES), jnp.int32),
            pltpu.VMEM((n_rows, PROFILE), F32),
            pltpu.VMEM((PROFILE * ROWS, LANES), F32),
            pltpu.VMEM((EXT, PROFILE + 8, LANES), F32),
            pltpu.VMEM((3, EXT, 24, LANES), F32),
            pltpu.VMEM((EXT, PROFILE, LANES), F32),
            pltpu.VMEM((3, EXT, 8, LANES), F32),
            pltpu.VMEM((3, EXT, FIELDS, 8, LANES), F32),
            pltpu.VMEM((2, 3, EXT, 8, LANES), F32),
            pltpu.VMEM((STEPS, EXT, 8, LANES), F32),
            pltpu.VMEM((ROWS, PROFILE, LANES), F32),
            pltpu.VMEM((cells, 2 * PROFILE), BF16),
            pltpu.VMEM((n_rows, cells), BF16),
            pltpu.VMEM((KINDS * PROFILE, 2 * PROFILE), BF16),
            pltpu.VMEM((KINDS * PROFILE, 2 * PROFILE), BF16),
            pltpu.VMEM((n_rows, KINDS * PROFILE), BF16),
            pltpu.VMEM((n_rows, KINDS * PROFILE), BF16),
            pltpu.VMEM((2 * PROFILE, n_rows), BF16),
            pltpu.SemaphoreType.DMA((7,)),
            pltpu.SemaphoreType.DMA((3,)),
            pltpu.SemaphoreType.DMA((2, 10)),
            pltpu.SemaphoreType.DMA((2, 2)),
            pltpu.SemaphoreType.DMA((2, 2, 3)),
            pltpu.SemaphoreType.DMA((2, 2)),
            pltpu.SemaphoreType.DMA((4,)),
            pltpu.SemaphoreType.DMA((4,)),
        ],
        compiler_params=pltpu.CompilerParams(collective_id=0, has_side_effects=True, vmem_limit_bytes=48 * 1024 * 1024),
        name="assimilate",
    )(
        increment.reshape(PROFILE * ROWS, LANES),
        coef_lon.reshape(FIELDS * ROWS, LANES),
        coef_lat.reshape(FIELDS * ROWS, LANES),
        obs_values,
        obs_weight,
        obs_operator,
        obs_columns.reshape(tiles, LANES),
        obs_types.reshape(tiles, LANES),
        obs_counts.reshape(1, n_lat),
    )
    return gradient.reshape(increment.shape), departures


def solution(mesh):
    return jax.shard_map(
        functools.partial(local, mesh.shape["lon"], mesh.shape["lat"]),
        mesh=mesh,
        in_specs=(
            P(None, None, "lat", "lon"),
            P(None, "lat", "lon"),
            P(None, "lat", "lon"),
            P(("lon", "lat"), None),
            P(("lon", "lat"), None),
            P(),
            P(("lon", "lat")),
            P(("lon", "lat")),
            P(("lon", "lat")),
        ),
        out_specs=(P(None, None, "lat", "lon"), P(("lon", "lat"), None)),
        check_vma=False,
    )
```

time: 443 us -> 82.9 us (0.19)
  waiting for transfers between devices: 208 us -> 0 us
  starting transfers between devices: 169 us -> 0 us
  Pallas kernels: 0 us -> 73.7 us
  other arithmetic: 25.7 us -> 0 us
  local copies, waits for them, and re-layouts: 32.5 us -> 7.47 us
    ppermute x40 -> x0, waiting for transfers between devices: 199 us -> none  [the longest x16 94.8 us: with_halo(): before = lax.ppermute(last, axis, up)]
    ppermute x40 -> x0, starting transfers between devices: 133 us -> none  [the longest x16 48.6 us: with_halo(): before = lax.ppermute(last, axis, up)]
    pallas_call x0 -> x1, Pallas kernels: none -> 73.7 us  [local(): pl.pallas_call(functools.partial(kernel, n_lon, n_lat, slots), out_shape=...]
    all_to_all x4 -> x0, starting transfers between devices: 35.8 us -> none  [the longest x1 14.1 us: local(): lax.all_to_all(slot_code, 'lat', split_axis=0, concat_axis=0, tiled=True)]
    scatter x10 -> x0, local copies, waits for them, and re-layouts: 22.1 us -> none  [spread_once(): padded_lat.at[:, :, 0, :].set(south_rim).at[:, :, -1, :].set(north_rim)]
    mul x22 -> x0, other arithmetic: 13.4 us -> none  [the longest x8 10.4 us: spread_once(): scaled_lon = root_lon * field_state]
    all_to_all x4 -> x0, waiting for transfers between devices: 8.37 us -> none  [the longest x1 8.36 us: local(): lax.all_to_all(obs_weight, 'lat', split_axis=0, concat_axis=0, tiled=True)]
  transfers between devices with their start and end apart: 44 -> 0, of which waited for: 21 -> 0; matrix products, arithmetic and copies ran while one was open for 12% -> 0% of each run, Pallas kernels for 0% -> 0%
where the time goes in v1:
time: 82.9 us; the launch traced here: 81.9 us
  Pallas kernels  73.7 us (89%)
  local copies, waits for them, and re-layouts  7.47 us (9%)
    pallas_call x1, Pallas kernels, local(): pl.pallas_call(functools.partial(kernel, n_lon, n_lat, slots), out_shape=...  73.7 us
    unnamed x20, local copies, waits for them, and re-layouts  7.47 us

profile of v1, /device:TPU:1, one launch (start us, length us, event | category | flops | bytes accessed | tf_op | source)
XLA Modules:
  0.0 81.9 jit_solution(11215479841021434041)
XLA Ops:
  0.6 0.0 copy-start.7
  0.6 0.0 copy-start.6
  0.7 0.0 copy-start.8
  0.7 0.7 copy-done.7
  1.3 0.0 copy-done.6
  1.3 0.0 copy-done.8
  1.3 0.0 copy-start
  1.3 1.0 %copy-done = f32[4,32,8,128]{3,2,1,0:T(8,128)S(1)} copy-done((f32[4,32,8,128]{3,2,1,0:T(8,128)S(1)}, f32[4,32,8,128]{3,2,1,0:T(8,128)}, u32[]{:S(2)}) %copy-start) | copy-done | bytes 524312
  2.4 0.0 copy-start.1
  2.4 0.9 %copy-done.1 = f32[512,128]{1,0:T(8,128)S(1)} copy-done((f32[512,128]{1,0:T(8,128)S(1)}, f32[512,128]{1,0:T(8,128)}, u32[]{:S(2)}) %copy-start.1) | copy-done | bytes 262168
  3.3 0.0 copy-start.2
  3.3 0.9 %copy-done.2 = f32[512,128]{1,0:T(8,128)S(1)} copy-done((f32[512,128]{1,0:T(8,128)S(1)}, f32[512,128]{1,0:T(8,128)}, u32[]{:S(2)}) %copy-start.2) | copy-done | bytes 262168
  4.3 0.0 copy-start.3
  4.3 0.9 %copy-done.3 = f32[3,128,128]{2,1,0:T(8,128)S(1)} copy-done((f32[3,128,128]{2,1,0:T(8,128)S(1)}, f32[3,128,128]{2,1,0:T(8,128)}, u32[]{:S(2)}) %copy-start.3) | copy-done | bytes 196632
  5.2 0.0 copy-start.4
  5.2 0.7 copy-done.4
  5.9 0.0 copy-start.5
  5.9 0.7 copy-done.5
  6.6 73.7 %assimilate.1 = (f32[1024,128]{1,0:T(8,128)S(1)}, f32[512,128]{1,0:T(8,128)S(1)}) custom-call(f32[1024,128]{1,0:T(8,128)S(1)} %bitcast.7, f32[32,128]{1,0:T(8,128)S(1)} %bitcast.9, f32[32,128]{1,0:T(8,128)S(1)} %bitcast.10, f32[512,128]{1,0:T(8,128)S(1)} %copy-done.1, f32[512,128]{1,0:T(8,128)S(1)} %copy-done.2, f32[3,128,128]{2,1,0:T(8,128)S(1)} %copy-done.3, ...), custom_call_target="tpu_custom_call" | custom-call | tf_op jit(solution)/shard_map/assimilate/pallas_call | solution.py:420
  80.4 0.8 copy.13
  81.2 0.7 copy.14
Async XLA Ops:
  0.6 0.7 copy-start.7
  0.6 0.7 copy-start.6
  0.7 0.7 copy-start.8
  1.3 1.0 %copy-start = (f32[4,32,8,128]{3,2,1,0:T(8,128)S(1)}, f32[4,32,8,128]{3,2,1,0:T(8,128)}, u32[]{:S(2)}) copy-start(f32[4,32,8,128]{3,2,1,0:T(8,128)} %param.9) | copy-start | bytes 1572868
  2.4 0.9 %copy-start.1 = (f32[512,128]{1,0:T(8,128)S(1)}, f32[512,128]{1,0:T(8,128)}, u32[]{:S(2)}) copy-start(f32[512,128]{1,0:T(8,128)} %obs_h.1) | copy-start | bytes 786436
  3.3 0.9 %copy-start.2 = (f32[512,128]{1,0:T(8,128)S(1)}, f32[512,128]{1,0:T(8,128)}, u32[]{:S(2)}) copy-start(f32[512,128]{1,0:T(8,128)} %wgt_h.1) | copy-start | bytes 786436
  4.3 0.9 %copy-start.3 = (f32[3,128,128]{2,1,0:T(8,128)S(1)}, f32[3,128,128]{2,1,0:T(8,128)}, u32[]{:S(2)}) copy-start(f32[3,128,128]{2,1,0:T(8,128)} %op_h.1) | copy-start | bytes 589828
  5.2 0.7 copy-start.4
  5.9 0.7 copy-start.5

commit v2 on v1

v2 whole, which is shorter than its diff:
```python
import functools

import jax
import jax.numpy as jnp
from jax import lax
from jax.experimental import pallas as pl
from jax.experimental.pallas import tpu as pltpu
from jax.sharding import PartitionSpec as P

HALO = 4
STEPS = 4
ROWS = 8
EXT = ROWS + 2 * HALO
LANES = 128
SPAN = LANES // 8
WIDE = SPAN + 2 * HALO
FIELDS = 4
PROFILE = 128
KINDS = 3
F32 = jnp.float32
BF16 = jnp.bfloat16
CORNER = ((1, 0, 3), (2, 3, 2), (3, 5, 1))


def lane_iota(shape):
    return lax.broadcasted_iota(jnp.int32, shape, len(shape) - 1)


def row_iota(shape):
    return lax.broadcasted_iota(jnp.int32, shape, 0)


def split(x):
    hi = x.astype(BF16)
    return hi, (x - hi.astype(F32)).astype(BF16)


def kernel(
    n_lon, n_lat, slots,
    inc_h, clon_h, clat_h, obs_h, wgt_h, op_h, col_h, typ_h, cnt_h,
    grad_o, dep_o,
    inc_v, cf_v, op_v, col_v, typ_v, cnt_v, obs_v, wgt_v, code_v, codes_in, codet_v, dep_v,
    xa, xe, ya, za, turn_v, rows_c, tile_v, tiles_in, side_v, corner_v, from_side, from_corner, relay_v,
    root_a, root_b, mid_c, lon_c, lat_c, st_v, oh_v, oht_v, opf_v, opb_v, lhs_hi, lhs_lo, adj_v,
    load_sem, own_sem, side_send, corner_send, tile_send, row_send, recv_side, recv_corner, recv_tile, recv_row, recv_coef,
    relay_send, relay_recv, a2a_send, a2a_recv,
):
    lon, lat = lax.axis_index("lon"), lax.axis_index("lat")
    n_rows = n_lat * slots
    n_tiles = n_rows // LANES
    per_tile = LANES // slots
    south, north = lat == 0, lat == n_lat - 1
    south_i, north_i = south.astype(jnp.int32), north.astype(jnp.int32)
    opposite = n_lon // 2

    def lon_at(by):
        return lax.rem(lon + by + n_lon, n_lon)

    def prev_of(d):
        return (lon_at(d + opposite * south_i), lat - 1 + south_i)

    def next_of(d):
        return (lon_at(d + opposite * north_i), lat + 1 - north_i)

    last, after = lax.rem(lon, opposite) == opposite - 1, lax.rem(lon, opposite) == 0
    last_i = last.astype(jnp.int32)

    def dev(where):
        return {"lon": where[0], "lat": where[1]}

    barrier = pltpu.get_barrier_semaphore()

    def greet(where):
        pl.semaphore_signal(barrier, inc=1, device_id=dev(where), device_id_type=pl.DeviceIdType.MESH)

    for d in (-1, 1):
        greet(prev_of(d))
        greet(next_of(d))
        greet((lon_at(d), lat))

    @pl.when(south)
    def _():
        greet(prev_of(0))

    @pl.when(north)
    def _():
        greet(next_of(0))

    @pl.when(last)
    def _():
        greet((lon_at(opposite), lat))

    @pl.when(after)
    def _():
        greet((lon_at(opposite - 1), lat))

    @pl.when(after & ~south)
    def _():
        greet((lon_at(opposite - 1), lat - 1))

    @pl.when(after & ~north)
    def _():
        greet((lon_at(opposite - 1), lat + 1))

    @pl.loop(1, n_lat)
    def _(k):
        greet((lon, lax.rem(lat + k, n_lat)))

    loads = [
        pltpu.make_async_copy(src, dst, load_sem.at[i])
        for i, (src, dst) in enumerate(
            (
                (inc_h, inc_v), (clon_h, cf_v.at[0]), (clat_h, cf_v.at[1]), (op_h, op_v),
                (col_h, col_v), (typ_h, typ_v), (cnt_h, cnt_v),
            )
        )
    ]
    for load in loads:
        load.start()
    mine = pl.ds(pl.multiple_of(lat * slots, slots), slots)
    own = [
        pltpu.make_async_copy(obs_h.at[mine], obs_v.at[mine], own_sem.at[0]),
        pltpu.make_async_copy(wgt_h.at[mine], wgt_v.at[mine], own_sem.at[1]),
    ]
    for copy in own:
        copy.start()

    for i in (4, 5, 6):
        loads[i].wait()
    rep = (lane_iota((n_lat, n_rows)) // slots == row_iota((n_lat, n_rows))).astype(F32).astype(BF16)
    counts = jnp.broadcast_to(cnt_v[...].astype(F32), (8, n_lat)).astype(BF16)
    limit = jnp.dot(counts, rep, preferred_element_type=F32)
    for q in range(n_tiles):
        lim = limit[0:1, q * LANES : (q + 1) * LANES].astype(jnp.int32)
        code = col_v[q : q + 1, :] * 4 + typ_v[q : q + 1, :] + 1
        code_v[q] = jnp.where(lane_iota((1, LANES)) % slots < lim, code, 0)

    for i in (0, 1, 2):
        loads[i].wait()

    @pl.loop(0, ROWS)
    def _(r):
        turn_v[r] = jnp.transpose(inc_v[pl.ds(r, PROFILE, stride=ROWS), :])
        for i in range(SPAN):
            xa[r + HALO, HALO + i] = turn_v[r, pl.ds(i, 8, stride=SPAN), :]
        for ct in range(2):
            rows_c[r + HALO, ct * FIELDS : (ct + 1) * FIELDS, :] = cf_v[ct, pl.ds(r, FIELDS, stride=ROWS), :]

    first, end = HALO, HALO + SPAN

    def stage(phase, x):
        for r in range(ROWS):
            for j in range(HALO):
                at = r % 2 * HALO + j
                side_v[phase, 0, r // 2, at : at + 1, :] = x[r + HALO, end - HALO + j, 7:8, :]
                side_v[phase, 1, r // 2, at : at + 1, :] = x[r + HALO, first + j, 0:1, :]
        for half in range(2):
            for k, at, n in CORNER:
                r = HALO + k - 1 if half == 0 else HALO + ROWS - k
                for j in range(n):
                    corner_v[phase, half, 0, at + j : at + j + 1, :] = x[r, end - n + j, 7:8, :]
                    corner_v[phase, half, 1, at + j : at + j + 1, :] = x[r, first + j, 0:1, :]

    stage(0, xa)
    lane = lane_iota((8, LANES))
    tile = jnp.zeros((8, LANES), F32)
    for r in range(ROWS):
        v = rows_c[r + HALO]
        tile = jnp.where(lane >> 2 == r, pltpu.roll(v, 4 * r + HALO, 1), tile)
        tile = jnp.where(lane >> 2 == r + 16, pltpu.roll(v, 64 + 4 * r, 1), tile)
    tile_v[0] = tile

    pl.semaphore_wait(barrier, n_lat - 1 + 6 + south_i + north_i + last_i * (4 - south_i - north_i))

    low, high = pl.ds(HALO, HALO), pl.ds(2 * HALO, HALO)
    inner = pl.ds(HALO, SPAN)
    to_prev = pl.ds(3 * HALO * (1 - south_i), HALO)
    to_next = pl.ds(3 * HALO * north_i, HALO)
    prev_side, next_side = 1 - south_i, north_i

    def send(src, dst, send_at, sem, where):
        return pltpu.make_async_remote_copy(
            src_ref=src, dst_ref=dst, send_sem=send_at, recv_sem=sem,
            device_id=dev(where), device_id_type=pl.DeviceIdType.MESH,
        )

    def start(copies):
        for copy in copies:
            copy.start()
        return copies

    class Routed:
        def __init__(self, other, plain, changed):
            self.other, self.plain, self.changed = other, plain, changed

        def start(self):
            pl.when(self.other)(self.changed.start)
            pl.when(~self.other)(self.plain.start)

        def wait_send(self):
            self.plain.wait_send()

    def by_relay(part, src, send_at):
        at = relay_v.at[pl.ds(*((0, 4), (4, 1), (5, 1), (6, 1))[part])]
        return send(src, at, send_at, relay_recv.at[part], (lon_at(opposite), lat))

    def small_copies(phase):
        copies = []
        for i, d in enumerate((1, -1)):
            src, send_at = side_v.at[phase, i], side_send.at[phase, i]
            copy = send(src, from_side.at[phase, i], send_at, recv_side.at[phase], (lon_at(d), lat))
            copies.append(copy if i or phase else Routed(last, copy, by_relay(0, src, send_at)))
            for half, side, where, pole in ((0, prev_side, prev_of(d), south), (1, next_side, next_of(d), north)):
                src, send_at = corner_v.at[phase, half, pl.ds(i, 1)], corner_send.at[phase, half, i]
                copy = send(src, from_corner.at[phase, side, pl.ds(i, 1)], send_at, recv_corner.at[phase], where)
                copies.append(copy if i or phase else Routed(last & ~pole, copy, by_relay(1 + half, src, send_at)))
        return copies

    def tile_copies():
        copies = []
        for i, d in enumerate((1, -1)):
            for v, (at, where, pole) in enumerate(
                ((2, (lon_at(d), lat), None), (prev_side, prev_of(d), south), (next_side, next_of(d), north))
            ):
                copy = send(tile_v, tiles_in.at[at, pl.ds(i, 1)], tile_send.at[v, i], recv_tile, where)
                if i == 0 and v == 0:
                    copy = Routed(last, copy, by_relay(3, tile_v, tile_send.at[v, i]))
                copies.append(copy if i or not v else Only(~last | pole, copy))
        return copies

    class Only:
        def __init__(self, holds, copy):
            self.holds, self.copy = holds, copy

        def start(self):
            pl.when(self.holds)(self.copy.start)

        def wait_send(self):
            pl.when(self.holds)(self.copy.wait_send)

    def pass_on():
        over = lon_at(1 - opposite)
        ways = [
            (last, 0, (0, 4), from_side.at[0, 0], recv_side.at[0], lat),
            (last & ~south, 1, (4, 1), from_corner.at[0, 1, pl.ds(0, 1)], recv_corner.at[0], lat - 1),
            (last & ~north, 2, (5, 1), from_corner.at[0, 0, pl.ds(0, 1)], recv_corner.at[0], lat + 1),
            (last, 3, (6, 1), tiles_in.at[2, pl.ds(0, 1)], recv_tile, lat),
            (last & ~south, None, (6, 1), tiles_in.at[1, pl.ds(0, 1)], recv_tile, lat - 1),
            (last & ~north, None, (6, 1), tiles_in.at[0, pl.ds(0, 1)], recv_tile, lat + 1),
        ]
        copies = []
        for n, (holds, part, (at, count), dst, sem, to) in enumerate(ways):
            src = relay_v.at[pl.ds(at, count)]
            copy = Only(holds, send(src, dst, relay_send.at[n], sem, (over, to)))
            if part is not None:
                arrived = pltpu.make_async_copy(src, src, relay_recv.at[part])
                pl.when(holds)(arrived.wait)
            copy.start()
            copies.append(copy)
        return copies

    def row_copies(phase, x):
        return [
            send(x.at[low, inner], x.at[to_prev, inner], row_send.at[phase, 0], recv_row.at[phase, prev_side], prev_of(0)),
            send(x.at[high, inner], x.at[to_next, inner], row_send.at[phase, 1], recv_row.at[phase, next_side], next_of(0)),
        ]

    def coef_copies():
        return [
            send(rows_c.at[low], rows_c.at[to_prev], row_send.at[2, 0], recv_coef.at[prev_side], prev_of(0)),
            send(rows_c.at[high], rows_c.at[to_next], row_send.at[2, 1], recv_coef.at[next_side], next_of(0)),
        ]

    def arrive(ref, sem):
        pltpu.make_async_copy(ref, ref, sem).wait()

    sent = start(small_copies(0) + tile_copies() + coef_copies())

    @pl.loop(1, n_lat)
    def _(k):
        to = lax.rem(lat + k, n_lat)
        pltpu.make_async_remote_copy(
            src_ref=code_v.at[to // per_tile], dst_ref=codes_in.at[lat], send_sem=a2a_send.at[0], recv_sem=a2a_recv.at[0],
            device_id=dev((lon, to)), device_id_type=pl.DeviceIdType.MESH,
        ).start()

    sent += start(row_copies(0, xa))

    @pl.loop(1, n_lat)
    def _(k):
        to = lax.rem(lat + k, n_lat)
        theirs = pl.ds(pl.multiple_of(to * slots, slots), slots)
        for i, (src, dst) in enumerate(((obs_h, obs_v), (wgt_h, wgt_v))):
            pltpu.make_async_remote_copy(
                src_ref=src.at[theirs], dst_ref=dst.at[mine], send_sem=a2a_send.at[1 + i], recv_sem=a2a_recv.at[1 + i],
                device_id=dev((lon, to)), device_id_type=pl.DeviceIdType.MESH,
            ).start()

    def all_but_one(ref, sem):
        part = ref.at[pl.ds(0, ref.shape[0] // n_lat * (n_lat - 1))]
        pltpu.make_async_copy(part, part, sem).wait()

    sent += pass_on()
    loads[3].wait()
    for k in range(KINDS):
        hi, lo = split(op_v[k])
        opf_v[k * PROFILE : (k + 1) * PROFILE, :] = jnp.concatenate([hi, lo], 1)
        hi, lo = split(jnp.transpose(op_v[k]))
        opb_v[k * PROFILE : (k + 1) * PROFILE, :] = jnp.concatenate([hi, lo], 1)

    def spread_profile(table, ct):
        return jnp.transpose(
            jnp.concatenate(
                [jnp.broadcast_to(table[ct * FIELDS + f : ct * FIELDS + f + 1, :], (PROFILE // FIELDS, LANES)) for f in range(FIELDS)], 0
            )
        )

    def ghosts(x, r):
        for j in range(HALO):
            x[r, j] = pltpu.roll(x[r, end - HALO + j], 1, 0)
            x[r, end + j] = pltpu.roll(x[r, first + j], 7, 0)

    def coefficients(r):
        table = rows_c[r]
        for ct, root in enumerate((root_a, root_b)):
            turn_v[ct] = spread_profile(table, ct)
            for i in range(SPAN):
                root[r, HALO + i] = turn_v[ct, pl.ds(i, 8, stride=SPAN), :]
            ghosts(root, r)

    def products(r, places):
        for i in places:
            a, b = root_a[r, i], root_b[r, i]
            mid_c[r, i] = 1.0 - 2.0 * (a * a + b * b)
            if i < WIDE - 1:
                lon_c[r, i] = a * root_a[r, i + 1]

    def products_lat(r, places):
        for i in places:
            lat_c[r, i] = root_b[r, i] * root_b[r + 1, i]

    @pl.loop(HALO, HALO + ROWS)
    def _(r):
        coefficients(r)
        ghosts(xa, r)

    all_but_one(codes_in, a2a_recv.at[0])
    codes_in[lat] = code_v[lat // per_tile]
    mod = lax.rem(lat, per_tile)
    lane_1 = lane_iota((1, LANES))
    for q in range(n_tiles):
        row = jnp.zeros((1, LANES), jnp.int32)
        for j in range(per_tile):
            moved = pltpu.roll(codes_in[q * per_tile + j], lax.rem(LANES + slots * (j - mod), LANES), 1)
            row = jnp.where(lane_1 // slots == j, moved, row)
        cell = (row - 1) >> 2
        cell = jnp.where(row > 0, (cell & -LANES) + (cell & (SPAN - 1)) * 8 + ((cell & (LANES - 1)) >> 4), -1)
        turned = jnp.transpose(jnp.broadcast_to(row.astype(F32), (LANES, LANES))).astype(jnp.int32)
        codet_v[q * LANES : (q + 1) * LANES, :] = turned
        across = jnp.transpose(jnp.broadcast_to(cell.astype(F32), (LANES, LANES))).astype(jnp.int32)
        down = jnp.broadcast_to(cell, (LANES, LANES))
        for r in range(ROWS):
            at = r * LANES
            oh_v[q * LANES : (q + 1) * LANES, at : at + LANES] = jnp.where(across == lane_iota((LANES, LANES)) + at, 1.0, 0.0).astype(BF16)
            oht_v[at : at + LANES, q * LANES : (q + 1) * LANES] = jnp.where(down == row_iota((LANES, LANES)) + at, 1.0, 0.0).astype(BF16)

    halo_rows = (0, 1, 2, 3, 12, 13, 14, 15)
    swaps = ((0, 3), (1, 2))
    for side in range(2):
        arrive(rows_c.at[pl.ds(3 * HALO * side, HALO)], recv_coef.at[side])
    for pole, base in ((south, 0), (north, 3 * HALO)):
        @pl.when(pole)
        def _():
            for p, q in swaps:
                one, two = rows_c[base + p], rows_c[base + q]
                rows_c[base + p] = two
                rows_c[base + q] = one

    @pl.loop(0, HALO)
    def _(r):
        coefficients(r)
        coefficients(r + 3 * HALO)

    @pl.loop(0, EXT)
    def _(r):
        products(r, range(HALO, HALO + SPAN))

    @pl.loop(0, EXT - 1)
    def _(r):
        products_lat(r, range(HALO, HALO + SPAN))

    arrive(tiles_in, recv_tile)
    side_tile = jnp.zeros((8, LANES), F32)
    for i in range(2):
        in_side = (lane >> 6) == i
        for e in range(EXT):
            if e < HALO:
                table, r = tiles_in[0, i], HALO + e - (1 + 2 * e) * south_i
            elif e < HALO + ROWS:
                table, r = tiles_in[2, i], e - HALO
            else:
                j = e - HALO - ROWS
                table, r = tiles_in[1, i], j + (ROWS - 1 - 2 * j) * north_i
            if HALO <= e < HALO + ROWS and e > HALO:
                continue
            if e == HALO:
                hit = in_side & ((lane & 63) >= 4 * HALO) & ((lane & 63) < 4 * (HALO + ROWS))
                side_tile = jnp.where(hit, pltpu.roll(table, 4 * HALO, 1), side_tile)
            else:
                moved = pltpu.roll(table, lax.rem(4 * (e - r) + LANES, LANES), 1)
                side_tile = jnp.where(in_side & ((lane & 63) >> 2 == e), moved, side_tile)
    for ct, root in enumerate((root_a, root_b)):
        turn_v[2 + ct] = spread_profile(side_tile, ct)
        for e in range(EXT):
            for j in range(HALO):
                root[e, j, 0:1, :] = turn_v[2 + ct, e * HALO + j : e * HALO + j + 1, :]
                root[e, end + j, 7:8, :] = turn_v[2 + ct, 64 + e * HALO + j : 65 + e * HALO + j, :]
    edge_places = (*range(HALO), *range(end, WIDE))

    @pl.loop(0, EXT)
    def _(r):
        products(r, (*edge_places, end - 1))

    @pl.loop(0, EXT - 1)
    def _(r):
        products_lat(r, edge_places)

    sign_south = jnp.where((lane >= LANES // 2) & south, -1.0, 1.0).astype(F32)
    sign_north = jnp.where((lane >= LANES // 2) & north, -1.0, 1.0).astype(F32)

    def complete(phase, x):
        for side, (pole, sign) in enumerate(((south, sign_south), (north, sign_north))):
            base = 3 * HALO * side
            arrive(x.at[pl.ds(base, HALO), inner], recv_row.at[phase, side])

            @pl.when(pole)
            def _():
                @pl.loop(first, end)
                def _(i):
                    for p, q in swaps:
                        one, two = x[base + p, i], x[base + q, i]
                        x[base + p, i] = two * sign
                        x[base + q, i] = one * sign

        @pl.loop(0, HALO)
        def _(r):
            ghosts(x, r)
            ghosts(x, r + 3 * HALO)

        arrive(from_side.at[phase], recv_side.at[phase])
        arrive(from_corner.at[phase], recv_corner.at[phase])
        for r in range(ROWS):
            for j in range(HALO):
                at = r % 2 * HALO + j
                x[r + HALO, j, 0:1, :] = from_side[phase, 0, r // 2, at : at + 1, :]
                x[r + HALO, end + j, 7:8, :] = from_side[phase, 1, r // 2, at : at + 1, :]
        for side, sign in enumerate((sign_south, sign_north)):
            west, east = from_corner[phase, side, 0] * sign, from_corner[phase, side, 1] * sign
            for k, at, n in CORNER:
                r = HALO - k if side == 0 else HALO + ROWS - 1 + k
                for j in range(n):
                    x[r, HALO - n + j, 0:1, :] = west[at + j : at + j + 1, :]
                    x[r, end + j, 7:8, :] = east[at + j : at + j + 1, :]

    def diffuse(x):
        for t, (src, dst) in enumerate(((x, ya), (ya, za), (za, ya), (ya, za))):
            @pl.loop(t + 1, EXT - 1 - t)
            def _(r):
                f = {i: src[r, i] for i in range(t, WIDE - t)}
                for i in range(t + 1, WIDE - 1 - t):
                    dst[r, i] = (
                        mid_c[r, i] * f[i]
                        + (lon_c[r, i - 1] * f[i - 1] + lon_c[r, i] * f[i + 1])
                        + (lat_c[r - 1, i] * src[r - 1, i] + lat_c[r, i] * src[r + 1, i])
                    )

    complete(0, xa)
    diffuse(xa)

    @pl.loop(0, ROWS)
    def _(r):
        v = za[r + HALO, first:end].reshape(LANES, PROFILE)
        hi, lo = split(v)
        st_v[pl.ds(pl.multiple_of(r * LANES, LANES), LANES), :] = jnp.concatenate([hi, lo], 1)

    found = jnp.dot(oh_v[...], st_v[...], preferred_element_type=F32)
    columns = found[:, :PROFILE] + found[:, PROFILE:]

    def by_kind(values, table):
        hi, lo = split(values)
        kind = (codet_v[...] - 1) & 3
        for k in range(KINDS):
            of_kind = kind == k
            lhs_hi[:, k * PROFILE : (k + 1) * PROFILE] = jnp.where(of_kind, hi.astype(F32), 0.0).astype(BF16)
            lhs_lo[:, k * PROFILE : (k + 1) * PROFILE] = jnp.where(of_kind, lo.astype(F32), 0.0).astype(BF16)
        one = jnp.dot(lhs_hi[...], table[...], preferred_element_type=F32)
        two = jnp.dot(lhs_lo[...], table[:, :PROFILE], preferred_element_type=F32)
        return one[:, :PROFILE] + one[:, PROFILE:] + two

    model = by_kind(columns, opf_v)
    for copy in own:
        copy.wait()
    all_but_one(obs_v, a2a_recv.at[1])
    all_but_one(wgt_v, a2a_recv.at[2])
    dep = jnp.where(codet_v[...] > 0, obs_v[...] - model, 0.0)
    dep_v[...] = dep
    adj = by_kind(wgt_v[...] * dep, opb_v)
    hi, lo = split(adj)
    adj_v[...] = jnp.concatenate([hi, lo], 1)
    forcing = jnp.dot(oht_v[...], adj_v[...], preferred_element_type=F32)
    forcing = forcing[:, :PROFILE] + forcing[:, PROFILE:]
    for r in range(ROWS):
        xe[r + HALO, first:end] = forcing[r * LANES : (r + 1) * LANES].reshape(SPAN, 8, PROFILE)
    stage(1, xe)
    sent += start(small_copies(1) + row_copies(1, xe))

    back = pltpu.make_async_copy(dep_v.at[mine], dep_o.at[mine], own_sem.at[2])
    back.start()

    @pl.loop(1, n_lat)
    def _(k):
        to = lax.rem(lat + k, n_lat)
        theirs = pl.ds(pl.multiple_of(to * slots, slots), slots)
        pltpu.make_async_remote_copy(
            src_ref=dep_v.at[theirs], dst_ref=dep_o.at[mine], send_sem=a2a_send.at[3], recv_sem=a2a_recv.at[3],
            device_id=dev((lon, to)), device_id_type=pl.DeviceIdType.MESH,
        ).start()

    @pl.loop(HALO, HALO + ROWS)
    def _(r):
        ghosts(xe, r)

    complete(1, xe)
    diffuse(xe)

    @pl.loop(0, ROWS)
    def _(r):
        for i in range(SPAN):
            turn_v[r, pl.ds(i, 8, stride=SPAN), :] = za[r + HALO, HALO + i]
        rows = pl.ds(r, PROFILE, stride=ROWS)
        grad_o[rows, :] = inc_v[rows, :] - jnp.transpose(turn_v[r])

    for copy in sent:
        copy.wait_send()
    all_but_one(codes_in, a2a_send.at[0])
    all_but_one(obs_v, a2a_send.at[1])
    all_but_one(wgt_v, a2a_send.at[2])
    all_but_one(dep_v, a2a_send.at[3])
    all_but_one(dep_o, a2a_recv.at[3])
    back.wait()


def local(n_lon, n_lat, increment, coef_lon, coef_lat, obs_values, obs_weight, obs_operator, obs_columns, obs_types, obs_counts):
    n_rows = obs_columns.shape[0]
    slots = n_rows // n_lat
    tiles = n_rows // LANES
    cells = ROWS * LANES
    vmem = pl.BlockSpec(memory_space=pltpu.VMEM)
    block = pltpu.VMEM((EXT, WIDE, 8, PROFILE), F32)
    gradient, departures = pl.pallas_call(
        functools.partial(kernel, n_lon, n_lat, slots),
        out_shape=(
            jax.ShapeDtypeStruct((PROFILE * ROWS, LANES), F32),
            jax.ShapeDtypeStruct((n_rows, PROFILE), F32),
        ),
        in_specs=[pl.BlockSpec(memory_space=pltpu.HBM)] * 9,
        out_specs=(vmem, vmem),
        scratch_shapes=[
            pltpu.VMEM((PROFILE * ROWS, LANES), F32),
            pltpu.VMEM((2, FIELDS * ROWS, LANES), F32),
            pltpu.VMEM((KINDS, PROFILE, PROFILE), F32),
            pltpu.VMEM((tiles, LANES), jnp.int32),
            pltpu.VMEM((tiles, LANES), jnp.int32),
            pltpu.VMEM((1, n_lat), jnp.int32),
            pltpu.VMEM((n_rows, PROFILE), F32),
            pltpu.VMEM((n_rows, PROFILE), F32),
            pltpu.VMEM((tiles, 1, LANES), jnp.int32),
            pltpu.VMEM((n_lat, 1, LANES), jnp.int32),
            pltpu.VMEM((n_rows, LANES), jnp.int32),
            pltpu.VMEM((n_rows, PROFILE), F32),
            block, block, block, block,
            pltpu.VMEM((ROWS, LANES, PROFILE), F32),
            pltpu.VMEM((EXT, 8, LANES), F32),
            pltpu.VMEM((1, 8, LANES), F32),
            pltpu.VMEM((3, 2, 8, LANES), F32),
            pltpu.VMEM((2, 2, 4, 8, PROFILE), F32),
            pltpu.VMEM((2, 2, 2, 8, PROFILE), F32),
            pltpu.VMEM((2, 2, 4, 8, PROFILE), F32),
            pltpu.VMEM((2, 2, 2, 8, PROFILE), F32),
            pltpu.VMEM((7, 8, PROFILE), F32),
            block, block, block, block, block,
            pltpu.VMEM((cells, 2 * PROFILE), BF16),
            pltpu.VMEM((n_rows, cells), BF16),
            pltpu.VMEM((cells, n_rows), BF16),
            pltpu.VMEM((KINDS * PROFILE, 2 * PROFILE), BF16),
            pltpu.VMEM((KINDS * PROFILE, 2 * PROFILE), BF16),
            pltpu.VMEM((n_rows, KINDS * PROFILE), BF16),
            pltpu.VMEM((n_rows, KINDS * PROFILE), BF16),
            pltpu.VMEM((n_rows, 2 * PROFILE), BF16),
            pltpu.SemaphoreType.DMA((7,)),
            pltpu.SemaphoreType.DMA((3,)),
            pltpu.SemaphoreType.DMA((2, 2)),
            pltpu.SemaphoreType.DMA((2, 2, 2)),
            pltpu.SemaphoreType.DMA((3, 2)),
            pltpu.SemaphoreType.DMA((3, 2)),
            pltpu.SemaphoreType.DMA((2,)),
            pltpu.SemaphoreType.DMA((2,)),
            pltpu.SemaphoreType.DMA,
            pltpu.SemaphoreType.DMA((2, 2)),
            pltpu.SemaphoreType.DMA((2,)),
            pltpu.SemaphoreType.DMA((6,)),
            pltpu.SemaphoreType.DMA((4,)),
            pltpu.SemaphoreType.DMA((4,)),
            pltpu.SemaphoreType.DMA((4,)),
        ],
        compiler_params=pltpu.CompilerParams(collective_id=0, has_side_effects=True, vmem_limit_bytes=56 * 1024 * 1024),
        name="assimilate",
    )(*(
        pltpu.with_memory_space_constraint(x, pltpu.HBM)
        for x in (
            increment.reshape(PROFILE * ROWS, LANES),
            coef_lon.reshape(FIELDS * ROWS, LANES),
            coef_lat.reshape(FIELDS * ROWS, LANES),
            obs_values,
            obs_weight,
            obs_operator,
            obs_columns.reshape(tiles, LANES),
            obs_types.reshape(tiles, LANES),
            obs_counts.reshape(1, n_lat),
        )
    ))
    return gradient.reshape(increment.shape), departures


def solution(mesh):
    return jax.shard_map(
        functools.partial(local, mesh.shape["lon"], mesh.shape["lat"]),
        mesh=mesh,
        in_specs=(
            P(None, None, "lat", "lon"),
            P(None, "lat", "lon"),
            P(None, "lat", "lon"),
            P(("lon", "lat"), None),
            P(("lon", "lat"), None),
            P(),
            P(("lon", "lat")),
            P(("lon", "lat")),
            P(("lon", "lat")),
        ),
        out_specs=(P(None, None, "lat", "lon"), P(("lon", "lat"), None)),
        check_vma=False,
    )
```

time: 82.9 us -> 61.1 us (0.74)
  Pallas kernels: 73.7 us -> 57.6 us
  local copies, waits for them, and re-layouts: 7.47 us -> 2.62 us
    pallas_call x1, Pallas kernels: 73.7 us -> 57.6 us  [local(): pl.pallas_call(functools.partial(kernel, n_lon, n_lat, slots), out_shape=...]
    unnamed x20 -> x4, local copies, waits for them, and re-layouts: 7.47 us -> 2.62 us
where the time goes in v2:
time: 61.1 us; the launch traced here: 60.9 us
  Pallas kernels  57.6 us (94%)
  local copies, waits for them, and re-layouts  2.62 us (4%)
  between operations  0.65 us (1%)
    pallas_call x1, Pallas kernels, local(): pl.pallas_call(functools.partial(kernel, n_lon, n_lat, slots), out_shape=...  57.6 us
    unnamed x4, local copies, waits for them, and re-layouts  2.62 us

profile of v2, /device:TPU:1, one launch (start us, length us, event | category | flops | bytes accessed | tf_op | source)
XLA Modules:
  0.0 60.9 jit_solution(13422918590507263602)
XLA Ops:
  0.6 57.6 %assimilate.1 = (f32[1024,128]{1,0:T(8,128)}, f32[512,128]{1,0:T(8,128)}) custom-call(f32[1024,128]{1,0:T(8,128)} %bitcast.7, f32[32,128]{1,0:T(8,128)} %bitcast.9, f32[32,128]{1,0:T(8,128)} %bitcast.10, f32[512,128]{1,0:T(8,128)} %obs_h.1, f32[512,128]{1,0:T(8,128)} %wgt_h.1, f32[3,128,128]{2,1,0:T(8,128)} %op_h.1, s32[4,128]{1,0:T(4,128)} %bitcast.11, ...), custom_call_target="tpu_custom_call" | custom-call | tf_op jit(solution)/shard_map/assimilate/pallas_call | solution.py:560
  58.3 0.0 copy-start
  58.3 1.9 %copy.13 = f32[4,32,8,128]{3,2,1,0:T(8,128)} copy(f32[4,32,8,128]{3,2,1,0:T(8,128)} %bitcast.8) | data formatting | bytes 1048576
  60.2 0.0 copy-done
  60.2 0.7 %copy.14 = f32[512,128]{1,0:T(8,128)} copy(f32[512,128]{1,0:T(8,128)S(1)} %copy-done) | data formatting | bytes 524288
Async XLA Ops:
  58.3 1.9 %copy-start = (f32[512,128]{1,0:T(8,128)S(1)}, f32[512,128]{1,0:T(8,128)}, u32[]{:S(2)}) copy-start(f32[512,128]{1,0:T(8,128)} %get-tuple-element.9) | copy-start | bytes 786436

commit v3 on v2

--- a/solution.py
+++ b/solution.py
@@ -43,7 +43,7 @@
     xa, xe, ya, za, turn_v, rows_c, tile_v, tiles_in, side_v, corner_v, from_side, from_corner, relay_v,
     root_a, root_b, mid_c, lon_c, lat_c, st_v, oh_v, oht_v, opf_v, opb_v, lhs_hi, lhs_lo, adj_v,
     load_sem, own_sem, side_send, corner_send, tile_send, row_send, recv_side, recv_corner, recv_tile, recv_row, recv_coef,
-    relay_send, relay_recv, a2a_send, a2a_recv,
+    relay_send, relay_recv, a2a_send, a2a_recv, ready_sem,
 ):
     lon, lat = lax.axis_index("lon"), lax.axis_index("lat")
     n_rows = n_lat * slots
@@ -63,7 +63,7 @@
         return (lon_at(d + opposite * north_i), lat + 1 - north_i)
 
     last, after = lax.rem(lon, opposite) == opposite - 1, lax.rem(lon, opposite) == 0
-    last_i = last.astype(jnp.int32)
+    last_i, after_i = last.astype(jnp.int32), after.astype(jnp.int32)
 
     def dev(where):
         return {"lon": where[0], "lat": where[1]}
@@ -73,10 +73,8 @@
     def greet(where):
         pl.semaphore_signal(barrier, inc=1, device_id=dev(where), device_id_type=pl.DeviceIdType.MESH)
 
-    for d in (-1, 1):
-        greet(prev_of(d))
-        greet(next_of(d))
-        greet((lon_at(d), lat))
+    for where in (prev_of(-1), next_of(-1), (lon_at(-1), lat)):
+        greet(where)
 
     @pl.when(south)
     def _():
@@ -92,6 +90,7 @@
 
     @pl.when(after)
     def _():
+        greet((lon_at(opposite), lat))
         greet((lon_at(opposite - 1), lat))
 
     @pl.when(after & ~south)
@@ -170,7 +169,11 @@
         tile = jnp.where(lane >> 2 == r + 16, pltpu.roll(v, 64 + 4 * r, 1), tile)
     tile_v[0] = tile
 
-    pl.semaphore_wait(barrier, n_lat - 1 + 6 + south_i + north_i + last_i * (4 - south_i - north_i))
+    pl.semaphore_wait(barrier, n_lat - 1 + 3 + south_i + north_i + last_i * (4 - south_i - north_i) + after_i)
+
+    for by, row in ((1, lat), (1 + opposite * south_i, lat - 1 + south_i), (1 + opposite * north_i, lat + 1 - north_i)):
+        by = jnp.where(last, 1 - opposite, by)
+        pl.semaphore_signal(ready_sem, inc=1, device_id=dev((lon_at(by), row)), device_id_type=pl.DeviceIdType.MESH)
 
     low, high = pl.ds(HALO, HALO), pl.ds(2 * HALO, HALO)
     inner = pl.ds(HALO, SPAN)
@@ -193,67 +196,77 @@
         def __init__(self, other, plain, changed):
             self.other, self.plain, self.changed = other, plain, changed
 
+        def ahead(self):
+            pl.when(self.other)(self.changed.start)
+
         def start(self):
-            pl.when(self.other)(self.changed.start)
             pl.when(~self.other)(self.plain.start)
 
         def wait_send(self):
             self.plain.wait_send()
 
-    def by_relay(part, src, send_at):
-        at = relay_v.at[pl.ds(*((0, 4), (4, 1), (5, 1), (6, 1))[part])]
-        return send(src, at, send_at, relay_recv.at[part], (lon_at(opposite), lat))
-
-    def small_copies(phase):
+    class Only:
+        def __init__(self, holds, copy):
+            self.holds, self.copy = holds, copy
+
+        def ahead(self):
+            pass
+
+        def start(self):
+            pl.when(self.holds)(self.copy.start)
+
+        def wait_send(self):
+            pl.when(self.holds)(self.copy.wait_send)
+
+    ends = (last, after)
+
+    def by_relay(i, part, src, send_at):
+        at = relay_v.at[i, pl.ds(*((0, 4), (4, 1), (5, 1), (6, 1))[part])]
+        return send(src, at, send_at, relay_recv.at[i, part], (lon_at(opposite), lat))
+
+    def small_copies(phase, *to):
         copies = []
-        for i, d in enumerate((1, -1)):
+        for i in to:
+            d = 1 - 2 * i
             src, send_at = side_v.at[phase, i], side_send.at[phase, i]
             copy = send(src, from_side.at[phase, i], send_at, recv_side.at[phase], (lon_at(d), lat))
-            copies.append(copy if i or phase else Routed(last, copy, by_relay(0, src, send_at)))
+            copies.append(copy if phase else Routed(ends[i], copy, by_relay(i, 0, src, send_at)))
             for half, side, where, pole in ((0, prev_side, prev_of(d), south), (1, next_side, next_of(d), north)):
                 src, send_at = corner_v.at[phase, half, pl.ds(i, 1)], corner_send.at[phase, half, i]
                 copy = send(src, from_corner.at[phase, side, pl.ds(i, 1)], send_at, recv_corner.at[phase], where)
-                copies.append(copy if i or phase else Routed(last & ~pole, copy, by_relay(1 + half, src, send_at)))
+                copies.append(copy if phase else Routed(ends[i] & ~pole, copy, by_relay(i, 1 + half, src, send_at)))
         return copies
 
-    def tile_copies():
+    def tile_copies(*to):
         copies = []
-        for i, d in enumerate((1, -1)):
+        for i in to:
+            d = 1 - 2 * i
             for v, (at, where, pole) in enumerate(
                 ((2, (lon_at(d), lat), None), (prev_side, prev_of(d), south), (next_side, next_of(d), north))
             ):
                 copy = send(tile_v, tiles_in.at[at, pl.ds(i, 1)], tile_send.at[v, i], recv_tile, where)
-                if i == 0 and v == 0:
-                    copy = Routed(last, copy, by_relay(3, tile_v, tile_send.at[v, i]))
-                copies.append(copy if i or not v else Only(~last | pole, copy))
+                if v == 0:
+                    copies.append(Routed(ends[i], copy, by_relay(i, 3, tile_v, tile_send.at[v, i])))
+                else:
+                    copies.append(Only(~ends[i] | pole, copy))
         return copies
 
-    class Only:
-        def __init__(self, holds, copy):
-            self.holds, self.copy = holds, copy
-
-        def start(self):
-            pl.when(self.holds)(self.copy.start)
-
-        def wait_send(self):
-            pl.when(self.holds)(self.copy.wait_send)
-
-    def pass_on():
-        over = lon_at(1 - opposite)
+    def pass_on(i):
+        over, end_of = lon_at((1 - opposite) * (1 - 2 * i)), ends[i]
         ways = [
-            (last, 0, (0, 4), from_side.at[0, 0], recv_side.at[0], lat),
-            (last & ~south, 1, (4, 1), from_corner.at[0, 1, pl.ds(0, 1)], recv_corner.at[0], lat - 1),
-            (last & ~north, 2, (5, 1), from_corner.at[0, 0, pl.ds(0, 1)], recv_corner.at[0], lat + 1),
-            (last, 3, (6, 1), tiles_in.at[2, pl.ds(0, 1)], recv_tile, lat),
-            (last & ~south, None, (6, 1), tiles_in.at[1, pl.ds(0, 1)], recv_tile, lat - 1),
-            (last & ~north, None, (6, 1), tiles_in.at[0, pl.ds(0, 1)], recv_tile, lat + 1),
+            (end_of, 0, (0, 4), from_side.at[0, i], recv_side.at[0], lat),
+            (end_of & ~south, 1, (4, 1), from_corner.at[0, 1, pl.ds(i, 1)], recv_corner.at[0], lat - 1),
+            (end_of & ~north, 2, (5, 1), from_corner.at[0, 0, pl.ds(i, 1)], recv_corner.at[0], lat + 1),
+            (end_of, 3, (6, 1), tiles_in.at[2, pl.ds(i, 1)], recv_tile, lat),
+            (end_of & ~south, None, (6, 1), tiles_in.at[1, pl.ds(i, 1)], recv_tile, lat - 1),
+            (end_of & ~north, None, (6, 1), tiles_in.at[0, pl.ds(i, 1)], recv_tile, lat + 1),
         ]
         copies = []
         for n, (holds, part, (at, count), dst, sem, to) in enumerate(ways):
-            src = relay_v.at[pl.ds(at, count)]
-            copy = Only(holds, send(src, dst, relay_send.at[n], sem, (over, to)))
+            src = relay_v.at[i, pl.ds(at, count)]
+            copy = Only(holds, send(src, dst, relay_send.at[i, n], sem, (over, to)))
             if part is not None:
-                arrived = pltpu.make_async_copy(src, src, relay_recv.at[part])
+                arrived = pltpu.make_async_copy(src, src, relay_recv.at[i, part])
                 pl.when(holds)(arrived.wait)
             copy.start()
             copies.append(copy)
@@ -274,7 +287,10 @@
     def arrive(ref, sem):
         pltpu.make_async_copy(ref, ref, sem).wait()
 
-    sent = start(small_copies(0) + tile_copies() + coef_copies())
+    eastward, westward = small_copies(0, 0) + tile_copies(0), small_copies(0, 1) + tile_copies(1)
+    for copy in eastward + westward:
+        copy.ahead()
+    sent = start(eastward + coef_copies())
 
     @pl.loop(1, n_lat)
     def _(k):
@@ -300,7 +316,6 @@
         part = ref.at[pl.ds(0, ref.shape[0] // n_lat * (n_lat - 1))]
         pltpu.make_async_copy(part, part, sem).wait()
 
-    sent += pass_on()
     loads[3].wait()
     for k in range(KINDS):
         hi, lo = split(op_v[k])
@@ -344,6 +359,7 @@
         coefficients(r)
         ghosts(xa, r)
 
+    sent += pass_on(0)
     all_but_one(codes_in, a2a_recv.at[0])
     codes_in[lat] = code_v[lat // per_tile]
     mod = lax.rem(lat, per_tile)
@@ -388,6 +404,9 @@
     @pl.loop(0, EXT - 1)
     def _(r):
         products_lat(r, range(HALO, HALO + SPAN))
+
+    pl.semaphore_wait(ready_sem, 3)
+    sent += start(westward) + pass_on(1)
 
     arrive(tiles_in, recv_tile)
     side_tile = jnp.zeros((8, LANES), F32)
@@ -512,7 +531,7 @@
     for r in range(ROWS):
         xe[r + HALO, first:end] = forcing[r * LANES : (r + 1) * LANES].reshape(SPAN, 8, PROFILE)
     stage(1, xe)
-    sent += start(small_copies(1) + row_copies(1, xe))
+    sent += start(small_copies(1, 0, 1) + row_copies(1, xe))
 
     back = pltpu.make_async_copy(dep_v.at[mine], dep_o.at[mine], own_sem.at[2])
     back.start()
@@ -587,7 +606,7 @@
             pltpu.VMEM((2, 2, 2, 8, PROFILE), F32),
             pltpu.VMEM((2, 2, 4, 8, PROFILE), F32),
             pltpu.VMEM((2, 2, 2, 8, PROFILE), F32),
-            pltpu.VMEM((7, 8, PROFILE), F32),
+            pltpu.VMEM((2, 7, 8, PROFILE), F32),
             block, block, block, block, block,
             pltpu.VMEM((cells, 2 * PROFILE), BF16),
             pltpu.VMEM((n_rows, cells), BF16),
@@ -608,10 +627,11 @@
             pltpu.SemaphoreType.DMA,
             pltpu.SemaphoreType.DMA((2, 2)),
             pltpu.SemaphoreType.DMA((2,)),
-            pltpu.SemaphoreType.DMA((6,)),
+            pltpu.SemaphoreType.DMA((2, 6)),
+            pltpu.SemaphoreType.DMA((2, 4)),
             pltpu.SemaphoreType.DMA((4,)),
             pltpu.SemaphoreType.DMA((4,)),
-            pltpu.SemaphoreType.DMA((4,)),
+            pltpu.SemaphoreType.REGULAR,
         ],
         compiler_params=pltpu.CompilerParams(collective_id=0, has_side_effects=True, vmem_limit_bytes=56 * 1024 * 1024),
         name="assimilate",

time: 61.1 us -> 56.7 us (0.928)
  Pallas kernels: 57.6 us -> 53.3 us
    pallas_call x1, Pallas kernels: 57.6 us -> 53.3 us  [local(): pl.pallas_call(functools.partial(kernel, n_lon, n_lat, slots), out_shape=...]
where the time goes in v3:
time: 56.7 us; the launch traced here: 56.6 us
  Pallas kernels  53.3 us (94%)
  local copies, waits for them, and re-layouts  2.62 us (5%)
  between operations  0.65 us (1%)
    pallas_call x1, Pallas kernels, local(): pl.pallas_call(functools.partial(kernel, n_lon, n_lat, slots), out_shape=...  53.3 us
    unnamed x4, local copies, waits for them, and re-layouts  2.62 us

profile of v3, /device:TPU:1, one launch (start us, length us, event | category | flops | bytes accessed | tf_op | source)
XLA Modules:
  0.0 56.6 jit_solution(7505788360108538117)
XLA Ops:
  0.6 53.3 %assimilate.1 = (f32[1024,128]{1,0:T(8,128)}, f32[512,128]{1,0:T(8,128)}) custom-call(f32[1024,128]{1,0:T(8,128)} %bitcast.7, f32[32,128]{1,0:T(8,128)} %bitcast.9, f32[32,128]{1,0:T(8,128)} %bitcast.10, f32[512,128]{1,0:T(8,128)} %obs_h.1, f32[512,128]{1,0:T(8,128)} %wgt_h.1, f32[3,128,128]{2,1,0:T(8,128)} %op_h.1, s32[4,128]{1,0:T(4,128)} %bitcast.11, ...), custom_call_target="tpu_custom_call" | custom-call | tf_op jit(solution)/shard_map/assimilate/pallas_call | solution.py:579
  53.9 0.0 copy-start
  54.0 1.9 %copy.13 = f32[4,32,8,128]{3,2,1,0:T(8,128)} copy(f32[4,32,8,128]{3,2,1,0:T(8,128)} %bitcast.8) | data formatting | bytes 1048576
  55.9 0.0 copy-done
  55.9 0.7 %copy.14 = f32[512,128]{1,0:T(8,128)} copy(f32[512,128]{1,0:T(8,128)S(1)} %copy-done) | data formatting | bytes 524288
Async XLA Ops:
  53.9 1.9 %copy-start = (f32[512,128]{1,0:T(8,128)S(1)}, f32[512,128]{1,0:T(8,128)}, u32[]{:S(2)}) copy-start(f32[512,128]{1,0:T(8,128)} %get-tuple-element.9) | copy-start | bytes 786436

commit v4 on v3

--- a/solution.py
+++ b/solution.py
@@ -526,6 +526,18 @@
     adj = by_kind(wgt_v[...] * dep, opb_v)
     hi, lo = split(adj)
     adj_v[...] = jnp.concatenate([hi, lo], 1)
+    def send_departures(begin, stop):
+        @pl.loop(begin, stop)
+        def _(k):
+            to = lax.rem(lat + k, n_lat)
+            theirs = pl.ds(pl.multiple_of(to * slots, slots), slots)
+            pltpu.make_async_remote_copy(
+                src_ref=dep_v.at[theirs], dst_ref=dep_o.at[mine], send_sem=a2a_send.at[3], recv_sem=a2a_recv.at[3],
+                device_id=dev((lon, to)), device_id_type=pl.DeviceIdType.MESH,
+            ).start()
+
+    early, late = n_lat * 3 // 8, n_lat * 5 // 8
+    send_departures(early, late)
     forcing = jnp.dot(oht_v[...], adj_v[...], preferred_element_type=F32)
     forcing = forcing[:, :PROFILE] + forcing[:, PROFILE:]
     for r in range(ROWS):
@@ -536,14 +548,8 @@
     back = pltpu.make_async_copy(dep_v.at[mine], dep_o.at[mine], own_sem.at[2])
     back.start()
 
-    @pl.loop(1, n_lat)
-    def _(k):
-        to = lax.rem(lat + k, n_lat)
-        theirs = pl.ds(pl.multiple_of(to * slots, slots), slots)
-        pltpu.make_async_remote_copy(
-            src_ref=dep_v.at[theirs], dst_ref=dep_o.at[mine], send_sem=a2a_send.at[3], recv_sem=a2a_recv.at[3],
-            device_id=dev((lon, to)), device_id_type=pl.DeviceIdType.MESH,
-        ).start()
+    send_departures(1, early)
+    send_departures(late, n_lat)
 
     @pl.loop(HALO, HALO + ROWS)
     def _(r):

time: 56.7 us -> 56.9 us (level)
  no operation moved by 1% of the time
where the time goes in v4:
time: 56.9 us; the launch traced here: 56.7 us
  Pallas kernels  53.5 us (94%)
  local copies, waits for them, and re-layouts  2.62 us (5%)
  between operations  0.65 us (1%)
    pallas_call x1, Pallas kernels, local(): pl.pallas_call(functools.partial(kernel, n_lon, n_lat, slots), out_shape=...  53.5 us
    unnamed x4, local copies, waits for them, and re-layouts  2.62 us

profile of v4, /device:TPU:1, one launch (start us, length us, event | category | flops | bytes accessed | tf_op | source)
XLA Modules:
  0.0 56.7 jit_solution(6619623431876186776)
XLA Ops:
  0.6 53.5 %assimilate.1 = (f32[1024,128]{1,0:T(8,128)}, f32[512,128]{1,0:T(8,128)}) custom-call(f32[1024,128]{1,0:T(8,128)} %bitcast.7, f32[32,128]{1,0:T(8,128)} %bitcast.9, f32[32,128]{1,0:T(8,128)} %bitcast.10, f32[512,128]{1,0:T(8,128)} %obs_h.1, f32[512,128]{1,0:T(8,128)} %wgt_h.1, f32[3,128,128]{2,1,0:T(8,128)} %op_h.1, s32[4,128]{1,0:T(4,128)} %bitcast.11, ...), custom_call_target="tpu_custom_call" | custom-call | tf_op jit(solution)/shard_map/assimilate/pallas_call | solution.py:585
  54.1 0.0 copy-start
  54.1 1.9 %copy.13 = f32[4,32,8,128]{3,2,1,0:T(8,128)} copy(f32[4,32,8,128]{3,2,1,0:T(8,128)} %bitcast.8) | data formatting | bytes 1048576
  56.0 0.0 copy-done
  56.0 0.7 %copy.14 = f32[512,128]{1,0:T(8,128)} copy(f32[512,128]{1,0:T(8,128)S(1)} %copy-done) | data formatting | bytes 524288
Async XLA Ops:
  54.1 1.9 %copy-start = (f32[512,128]{1,0:T(8,128)S(1)}, f32[512,128]{1,0:T(8,128)}, u32[]{:S(2)}) copy-start(f32[512,128]{1,0:T(8,128)} %get-tuple-element.9) | copy-start | bytes 786436
